TPU v7x, 256 devices: a whole 4x4x8 slice. The times are simulated.
256 devices in a mesh: req: 64 (over x_lo, z, y), tp: 4 (over x_hi, core).
Axes of the slice: x: 4 (x_hi: 2, x_lo: 2; x = x_hi * 2 + x_lo), y: 4, z: 8, core: 2. Of those that a mesh axis runs over, the one named last changes fastest.
Arguments:
- hidden: bfloat16 [64, 512, 1280], P('req'), may hold values from -6 to 6
- membership: int32 [64], P('req'), may hold values from 0 to 3
- lengths: int32 [64], P('req'), may hold values from 8 to 512, as said below
- owners: int32 [4, 16], replicated, may hold values from 0 to 63, as said below
- prefix_cache: bfloat16 [4096, 20, 128], P('req', 'tp'), may hold values from -6 to 6
- w_query: bfloat16 [1280, 1280], P(None, 'tp'), may hold values from -0.25 to 0.25
- w_key: bfloat16 [1280, 1280], P(None, 'tp'), may hold values from -0.25 to 0.25
- w_value: bfloat16 [1280, 1280], P(None, 'tp'), may hold values from -0.15625 to 0.15625
- key_scale: float32 [20, 64], P('tp'), may hold values from 0.5 to 6
- w_out: bfloat16 [1280, 1280], P('tp'), may hold values from -0.15625 to 0.15625
- step_rates: float32 [1280], replicated, may hold values from 0.1 to 0.8
Outputs:
- layer_out: bfloat16 [64, 512, 1280], P('req', None, 'tp')
Inputs may be any that keep to these rules, and one draw needn't show every extreme that they name: `lengths`: every request has at least one suffix token; some request has length 512. `owners`: each cache slot appears exactly once in the table.
All inputs are finite; a program needn't handle non-finite values.
Results may differ from a plain program's by a relative error of at most 0.0085.
Values may be sent and summed in bfloat16 or wider, within the bound.
No kernel may reach another device: no remote copies, remote signals or barrier semaphores. Data moves between devices by JAX's collectives and lax.ppermute only.
A program may use at most 128 MiB of HBM per device.

v0:
```python
import math

import jax
import jax.numpy as jnp
import numpy as np
from jax import lax
from jax.experimental import pallas as pl
from jax.experimental.pallas import tpu as pltpu
from jax.sharding import PartitionSpec as P


F32 = jnp.float32
BF16 = jnp.bfloat16
LOG2E = math.log2(math.e)
EPS = 1e-06

NX, NZ, NY = 2, 8, 4


def add3(a, b):
    return ((a[0] + b[0]) % NX, (a[1] + b[1]) % NZ, (a[2] + b[2]) % NY)


def flat3(a):
    return a[0] * NZ * NY + a[1] * NY + a[2]


def unflat3(i):
    return (i // (NZ * NY), (i // NY) % NZ, i % NY)


def fetch(array, offset):
    pairs = [(flat3(add3(unflat3(i), offset)), i) for i in range(NX * NZ * NY)]
    return lax.ppermute(array, "req", pairs)


QUAD = ((0, 0, 0), (1, 0, 0), (0, 4, 0), (1, 4, 0))
HALVES = (
    dict(
        pool=((0, 0, 0), (0, 1, 0), (0, 7, 0), (0, 6, 0)),
        near=((0, 0, 1), (0, 0, 3), (0, 0, 2)),
        sends=((0, 0, 1), (0, 0, 3), (0, 0, 2)),
    ),
    dict(
        pool=((0, 0, 0), (0, 0, 1), (0, 0, 3), (0, 0, 2)),
        near=((0, 1, 0), (0, 7, 0), (0, 2, 0)),
        sends=((0, 1, 0), (0, 7, 0), (0, 2, 0), (0, 6, 0)),
    ),
)
CAP = 8
CHUNKS = 2


def minus3(a):
    return (-a[0] % NX, -a[1] % NZ, -a[2] % NY)


def place_table(half):
    pool = [add3(p, q) for p in half["pool"] for q in QUAD]
    order = [add3(n, m) for n in ((0, 0, 0),) + half["near"] for m in pool]
    assert sorted(flat3(m) for m in order) == list(range(64))
    table = np.zeros(64, np.int32)
    for place, m in enumerate(order):
        table[flat3(m)] = place
    return table


def member_spot(target):
    for n, half in enumerate(HALVES):
        for k, p in enumerate(half["pool"]):
            for b, q in enumerate(QUAD):
                if add3(p, q) == target:
                    return n, k, b
    raise ValueError(target)


def dot_t(a, b):
    return lax.dot_general(a, b, (((1,), (1,)), ((), ())), preferred_element_type=F32)


def pair_lanes(scale, fill):
    return jnp.concatenate([scale, jnp.full_like(scale, fill)], axis=1)


def lane_half(lanes):
    return lax.broadcasted_iota(jnp.int32, (1, lanes), 1) < lanes // 2


def prep_kernel(member_ref, block_ref, scale_ref, flag_ref, whole_ref):
    heads, rows, lanes = block_ref.shape
    size = lanes // 2
    first = lane_half(lanes)
    scale = scale_ref[...]
    bound = jnp.max(scale * scale) * (1.02 * LOG2E * math.sqrt(size))
    flag_ref[0] = (bound <= 60.0).astype(jnp.int32)
    for h in range(heads):
        wide = block_ref[h].astype(F32)
        mean = jnp.sum(jnp.where(first, wide * wide, 0.0), axis=-1, keepdims=True) * (1.0 / size)
        keys = wide * lax.rsqrt(mean + EPS) * pair_lanes(scale[h : h + 1], 1.0)
        whole_ref[h] = jnp.where(first, keys, wide).astype(BF16)
    whole_ref[heads] = jnp.full((rows, lanes), member_ref[0].astype(F32)).astype(BF16)


def qkv_kernel(hid_ref, wq_ref, wk_ref, wv_ref, scale_ref, q_ref, kv_ref, w_ref, *, tile):
    heads, suf, lanes = q_ref.shape
    size = lanes // 2
    first = lane_half(lanes)
    for h in range(heads):
        own = slice(h * size, (h + 1) * size)
        w_ref[h, :size] = wq_ref[own]
        w_ref[h, size : 2 * size] = jnp.zeros_like(wq_ref[own])
        w_ref[h, 2 * size : 3 * size] = wk_ref[own]
        w_ref[h, 3 * size :] = wv_ref[own]
    for h in range(heads):
        scale = scale_ref[h : h + 1]
        q_scale = pair_lanes(scale * (LOG2E / math.sqrt(size)), 0.0)
        k_scale = pair_lanes(scale, 1.0)
        for i in range(suf // tile):
            rows = slice(i * tile, (i + 1) * tile)
            both = dot_t(hid_ref[rows], w_ref[h])
            q, kv = both[:, :lanes], both[:, lanes:]
            q_mean = jnp.sum(q * q, axis=-1, keepdims=True) * (1.0 / size)
            k_mean = jnp.sum(jnp.where(first, kv * kv, 0.0), axis=-1, keepdims=True) * (1.0 / size)
            q_ref[h, rows] = (q * lax.rsqrt(q_mean + EPS) * q_scale).astype(BF16)
            keys = kv * lax.rsqrt(k_mean + EPS) * k_scale
            kv_ref[h, rows] = jnp.where(first, keys, kv).astype(BF16)


def suffix_kernel(len_ref, flag_ref, q_ref, kv_ref, acc_ref, peak_ref, *, tile):
    heads, suf, lanes = q_ref.shape
    first = lane_half(lanes)
    length = len_ref[0]
    safe = flag_ref[0] == 1

    @pl.when(safe)
    def _():
        qpos = lax.broadcasted_iota(jnp.int32, (tile, tile), 0)
        kpos = lax.broadcasted_iota(jnp.int32, (tile, tile), 1)
        masks = []
        for j in range(suf // tile):
            inside = kpos + j * tile < length
            masks.append((inside & (kpos <= qpos), inside))
        for h in range(heads):
            for i in range(suf // tile):
                rows = slice(i * tile, (i + 1) * tile)
                total = None
                for j in range(i + 1):
                    keys = kv_ref[h, j * tile : (j + 1) * tile]
                    weights = jnp.exp2(dot_t(q_ref[h, rows], keys))
                    weights = jnp.where(masks[j][0 if i == j else 1], weights, 0.0).astype(BF16)
                    ones_values = jnp.where(first, jnp.ones_like(keys), keys)
                    part = jnp.dot(weights, ones_values, preferred_element_type=F32)
                    total = part if total is None else total + part
                acc_ref[h, rows] = total

    @pl.when(jnp.logical_not(safe))
    def _():
        lane = lax.broadcasted_iota(jnp.int32, (1, lanes), 1)
        peak_ref[...] = jnp.zeros_like(peak_ref)

        def head(h, carry):
            for i in range(suf // tile):
                rows = slice(i * tile, (i + 1) * tile)
                count = (i + 1) * tile
                qpos = lax.broadcasted_iota(jnp.int32, (tile, count), 0) + i * tile
                kpos = lax.broadcasted_iota(jnp.int32, (tile, count), 1)
                keys = kv_ref[h, :count]
                scores = jnp.where(
                    (kpos <= qpos) & (kpos < length), dot_t(q_ref[h, rows], keys), -1e30
                )
                peak = jnp.max(scores, axis=-1, keepdims=True)
                weights = jnp.exp2(scores - peak).astype(BF16)
                ones_values = jnp.where(first, jnp.ones_like(keys), keys)
                acc_ref[h, rows] = jnp.dot(weights, ones_values, preferred_element_type=F32)
                peak_ref[rows] = jnp.where(lane == h, peak, peak_ref[rows])
            return carry

        lax.fori_loop(0, heads, head, 0)


def split_kernel(a_ref, b_ref, c_ref, d_ref, one_ref, two_ref):
    rows = one_ref.shape[2]
    for n, ref in enumerate((a_ref, b_ref, c_ref, d_ref)):
        one_ref[n] = ref[:, :rows]
        two_ref[n] = ref[:, rows:]


def plan_kernel(member_ref, place_ref, owners_ref, table_ref, send_ref, recv_ref, over_ref, count_ref):
    group = member_ref[0]
    me = place_ref[0]
    groups, slots = owners_ref.shape

    def spots(owner):
        rel = (
            ((owner ^ me) & 32)
            + ((((owner >> 2) - (me >> 2)) & 7) << 2)
            + ((owner - me) & 3)
        )
        return table_ref[rel], table_ref[64 + rel]

    def by_group(g, most):
        for n in range(8):
            count_ref[n] = 0

        def by_slot(j, carry):
            most, held = carry
            owner = owners_ref[g, j]
            after = []
            for half, (spot, color) in enumerate(zip(spots(owner), (owner & 3, (owner >> 2) & 3))):
                send_ref[half * 64 + g * slots + held[half]] = spot
                after.append(held[half] + (spot < 16).astype(jnp.int32))
                seen = count_ref[half * 4 + color] + 1
                count_ref[half * 4 + color] = seen
                most = jnp.maximum(most, seen)
            return most, tuple(after)

        return lax.fori_loop(0, slots, by_slot, (most, (jnp.int32(0), jnp.int32(0))))[0]

    most = lax.fori_loop(0, groups, by_group, jnp.int32(0))
    over_ref[0] = (most > CAP).astype(jnp.int32)
    for n in range(8):
        count_ref[n] = 0

    def by_own(j, carry):
        for half, spot in enumerate(spots(owners_ref[group, j])):
            source = spot >> 4
            rank = count_ref[half * 4 + source]
            count_ref[half * 4 + source] = rank + 1
            recv_ref[half * slots + j] = source * 16 + rank
        return carry

    lax.fori_loop(0, slots, by_own, 0)


def pack_kernel(member_ref, send_ref, *rest, start):
    quads, outs, pool_ref = (rest[:4], rest[4:8]), rest[8:-1], rest[-1]
    heads = pool_ref.shape[2]
    for half in range(2):
        for n in range(4):
            pool_ref[half, 4 * n : 4 * n + 4] = quads[half][n][:, :heads]

    def wanted(target):
        n, k, b = member_spot(target)
        value = quads[n][k][b, heads].astype(F32)
        return jnp.max(value).astype(jnp.int32)

    jobs = []
    place = 0
    for n, half in enumerate(HALVES):
        if start == 0:
            jobs.append((outs[place], n, member_ref[0], 0))
            place += 1
        for k, offset in enumerate(half["sends"]):
            out = outs[place]
            place += 1
            jobs.append((out, n, wanted(minus3(offset)), start + (out.shape[0] if k == 3 else 0)))
    for out, half, group, first in jobs:

        def copy(i, carry, out=out, half=half, group=group, first=first):
            spot = send_ref[half * 64 + group * 16 + first + i] & 15
            out[i] = pool_ref[half, spot]
            return carry

        lax.fori_loop(0, out.shape[0], copy, 0)


def select_kernel(recv_ref, *rest):
    kv_ref, sems = rest[-2:]
    blocks = rest[:-2]
    slots = recv_ref.shape[0] // 2
    part = kv_ref.shape[1] // (2 * slots)
    spots = []
    for start in range(0, CAP * (2 if len(blocks) > 9 else 1), CAP):
        for n, half in enumerate(HALVES):
            if start == 0:
                spots.append((n, 0, 0))
            for k in range(len(half["sends"])):
                spots.append((n, min(k, 2) + 1, start + (CAP // 2 if k == 3 else 0)))
    assert len(spots) == len(blocks)

    def begin(j, carry):
        for half in range(2):
            code = recv_ref[half * slots + j]
            row = pl.multiple_of((2 * j + half) * part, part)
            goal = kv_ref.at[:, pl.ds(row, part), :]
            for ref, (n, source, low) in zip(blocks, spots):
                if n != half:
                    continue
                least = source * 16 + low

                @pl.when((code >= least) & (code < least + ref.shape[0]))
                def _(ref=ref, least=least):
                    pltpu.make_async_copy(ref.at[code - least], goal, sems.at[2 * j + half]).start()

        return carry

    lax.fori_loop(0, slots, begin, 0)

    def finish(j, carry):
        row = pl.multiple_of(j * part, part)
        goal = kv_ref.at[:, pl.ds(row, part), :]
        pltpu.make_async_copy(blocks[0].at[0], goal, sems.at[j]).wait()
        return carry

    lax.fori_loop(0, 2 * slots, finish, 0)


def attend_kernel(flag_ref, q_ref, acc_ref, peak_ref, kv_ref, out_ref, total_ref, *, tile):
    heads, _, lanes = q_ref.shape
    size = lanes // 2
    count = kv_ref.shape[1]
    first = lane_half(lanes)
    safe = flag_ref[0] == 1

    @pl.when(safe)
    def _():
        for h in range(heads):
            total = acc_ref[h]
            for j in range(count // tile):
                keys = kv_ref[h, j * tile : (j + 1) * tile]
                weights = jnp.exp2(dot_t(q_ref[h], keys)).astype(BF16)
                ones_values = jnp.where(first, jnp.ones_like(keys), keys)
                total = total + jnp.dot(weights, ones_values, preferred_element_type=F32)
            total_ref[h] = total

    @pl.when(jnp.logical_not(safe))
    def _():
        lane = lax.broadcasted_iota(jnp.int32, (1, lanes), 1)

        def head(h, carry):
            keys = kv_ref[h]
            scores = dot_t(q_ref[h], keys)
            near = jnp.max(jnp.where(lane == h, peak_ref[...], -3e38), axis=-1, keepdims=True)
            peak = jnp.maximum(jnp.max(scores, axis=-1, keepdims=True), near)
            weights = jnp.exp2(scores - peak).astype(BF16)
            ones_values = jnp.where(first, jnp.ones_like(keys), keys)
            total = jnp.dot(weights, ones_values, preferred_element_type=F32)
            total_ref[h] = total + acc_ref[h] * jnp.exp2(near - peak)
            return carry

        lax.fori_loop(0, heads, head, 0)

    for h in range(heads):
        total = total_ref[h]
        value = total / pltpu.roll(total, size, 1)
        out_ref[:, h * size : (h + 1) * size] = value[:, size:].astype(BF16)


def output_kernel(
    len_ref, rank_ref, a0, a1, a2, a3, w0, w1, w2, w3, hid_ref, rate_ref, *rest, tile, start
):
    out_ref, moved_ref = rest[-2:]
    count, width = hid_ref.shape
    part = out_ref.shape[0]
    length = len_ref[0]
    rank = rank_ref[0]
    cols = [slice(n * tile, (n + 1) * tile) for n in range(width // tile)]
    square = None
    for col in cols:
        branch = jnp.dot(a0[...], w0[:, col], preferred_element_type=F32)
        for a, w in ((a1, w1), (a2, w2), (a3, w3)):
            branch += jnp.dot(a[...], w[:, col], preferred_element_type=F32)
        moved_ref[:, col] = branch
        part_square = jnp.sum(branch * branch, axis=-1, keepdims=True)
        square = part_square if square is None else square + part_square
    gain = lax.rsqrt(square * (1.0 / width) + EPS)
    square = None
    for col in cols:
        state = hid_ref[:, col].astype(F32)
        moved = state + rate_ref[:, col] * (moved_ref[:, col] * gain - state)
        moved_ref[:, col] = moved
        part_square = jnp.sum(moved * moved, axis=-1, keepdims=True)
        square = part_square if square is None else square + part_square
    norm = lax.rsqrt(square * (1.0 / width) + EPS)
    pos = lax.broadcasted_iota(jnp.int32, (count, 1), 0) + start
    for t in range(width // part):

        @pl.when(rank == t)
        def _(t=t):
            mine = moved_ref[:, t * part : (t + 1) * part]
            out_ref[...] = jnp.where(pos < length, mine * norm, 0.0).T.astype(BF16)


VMEM = pl.BlockSpec(memory_space=pltpu.VMEM)
SMEM = pl.BlockSpec(memory_space=pltpu.SMEM)
ANY = pl.BlockSpec(memory_space=pl.ANY)


def across(array, bit):
    return lax.ppermute(array, "tp", [(i, i ^ bit) for i in range(4)])


def shaped(shape, dtype):
    return jax.ShapeDtypeStruct(shape, dtype)


def vmem(mebibytes):
    return pltpu.CompilerParams(vmem_limit_bytes=mebibytes << 20)


def cost(flops, exps, moved):
    return pl.CostEstimate(flops=flops, transcendentals=exps, bytes_accessed=moved)


def gather_prefix(whole, membership, owners):
    planes, rows, lanes = whole.shape
    heads, part, slots = planes - 1, rows // 2, owners.shape[1]
    place = lax.axis_index("req").astype(jnp.int32).reshape(1)
    table = jnp.asarray(np.concatenate([place_table(half) for half in HALVES]))
    send, recv, over = pl.pallas_call(
        plan_kernel,
        out_shape=(shaped((128,), jnp.int32), shaped((2 * slots,), jnp.int32), shaped((1,), jnp.int32)),
        in_specs=[SMEM] * 4,
        out_specs=(SMEM,) * 3,
        scratch_shapes=[pltpu.SMEM((8,), jnp.int32)],
        name="plan",
        compiler_params=vmem(1),
        cost_estimate=cost(0, 0, 1_000_000),
    )(membership, place, owners, table)
    quads = pl.pallas_call(
        split_kernel,
        out_shape=(shaped((4, planes, part, lanes), BF16),) * 2,
        in_specs=[VMEM] * 4,
        out_specs=(VMEM, VMEM),
        name="split",
        compiler_params=vmem(2),
        cost_estimate=cost(0, 0, 600_000),
    )(whole, *[fetch(whole, offset) for offset in QUAD[1:]])
    held = []
    for quad, half in zip(quads, HALVES):
        held += [quad] + [fetch(quad, offset) for offset in half["pool"][1:]]

    def one_round(start):
        shapes, offsets = [], []
        for half in HALVES:
            if start == 0:
                shapes.append(16)
                offsets.append(None)
            for offset in half["sends"]:
                shapes.append(CAP // 2 if len(half["sends"]) == 4 and offset[1] in (2, 6) else CAP)
                offsets.append(offset)
        packed = pl.pallas_call(
            lambda *refs: pack_kernel(*refs, start=start),
            out_shape=tuple(shaped((n, heads, part, lanes), BF16) for n in shapes),
            in_specs=[SMEM] * 2 + [VMEM] * 8,
            out_specs=(VMEM,) * len(shapes),
            scratch_shapes=[pltpu.VMEM((2, 16, heads, part, lanes), BF16)],
            name="pack",
            compiler_params=vmem(8),
            cost_estimate=cost(0, 0, 4_000_000),
        )(membership, send, *held)
        return [a if o is None else fetch(a, o) for a, o in zip(packed, offsets)]

    def select(arrays):
        return pl.pallas_call(
            select_kernel,
            out_shape=shaped((heads, slots * rows, lanes), BF16),
            in_specs=[SMEM] + [ANY] * len(arrays),
            out_specs=VMEM,
            scratch_shapes=[pltpu.SemaphoreType.DMA((2 * slots,))],
            name="select",
            compiler_params=vmem(4),
            cost_estimate=cost(0, 0, 3_000_000),
        )(recv, *arrays)

    arrays = one_round(0)
    prefix = lax.cond(
        over[0] > 0,
        lambda: select(arrays + one_round(CAP)),
        lambda: select(arrays),
    )
    return prefix


def local(
    hidden,
    membership,
    lengths,
    owners,
    prefix_cache,
    w_query,
    w_key,
    w_value,
    key_scale,
    w_out,
    step_rates,
):
    _, suf, width = hidden.shape
    heads, size = key_scale.shape
    lanes = 2 * size
    slot_rows = prefix_cache.shape[0]
    rows = hidden.reshape(suf, width)
    flag, whole = pl.pallas_call(
        prep_kernel,
        out_shape=(shaped((1,), jnp.int32), shaped((heads + 1, slot_rows, lanes), BF16)),
        in_specs=[SMEM, VMEM, VMEM],
        out_specs=(SMEM, VMEM),
        name="prep",
        compiler_params=vmem(2),
        cost_estimate=cost(0, 0, 300_000),
    )(membership, jnp.transpose(prefix_cache, (1, 0, 2)), key_scale)
    prefix = gather_prefix(whole, membership, owners)
    w_far = across(w_out, 2)
    q, kv = pl.pallas_call(
        lambda *refs: qkv_kernel(*refs, tile=256),
        out_shape=(shaped((heads, suf, lanes), BF16),) * 2,
        in_specs=[VMEM] * 5,
        out_specs=(VMEM, VMEM),
        scratch_shapes=[pltpu.VMEM((heads, 2 * lanes, width), BF16)],
        name="qkv",
        compiler_params=vmem(14),
        cost_estimate=cost(2 * suf * width * 3 * heads * size, 0, 10_000_000),
    )(rows, w_query.T, w_key.T, w_value.T, key_scale)
    acc, peaks = pl.pallas_call(
        lambda *refs: suffix_kernel(*refs, tile=256),
        out_shape=(shaped((heads, suf, lanes), F32), shaped((suf, lanes), F32)),
        in_specs=[SMEM, SMEM, VMEM, VMEM],
        out_specs=(VMEM, VMEM),
        name="suffix",
        compiler_params=vmem(10),
        cost_estimate=cost(4 * suf * suf * heads * lanes, suf * suf * heads, 10_000_000),
    )(lengths, flag, q, kv)
    w_core = across(w_out, 1)
    w_both = across(w_far, 1)
    prefix_rows = prefix.shape[1]
    part = width // 4
    rank = lax.axis_index("tp").astype(jnp.int32).reshape(1)
    chunk = suf // CHUNKS
    attended = []
    for c in range(CHUNKS):
        attended.append(
            pl.pallas_call(
                lambda *refs: attend_kernel(*refs, tile=256),
                grid=(1,),
                out_shape=shaped((chunk, heads * size), BF16),
                in_specs=[
                    SMEM,
                    pl.BlockSpec((heads, chunk, lanes), lambda i, c=c: (0, c, 0)),
                    pl.BlockSpec((heads, chunk, lanes), lambda i, c=c: (0, c, 0)),
                    pl.BlockSpec((chunk, lanes), lambda i, c=c: (c, 0)),
                    VMEM,
                ],
                out_specs=pl.BlockSpec((chunk, heads * size), lambda i: (0, 0)),
                scratch_shapes=[pltpu.VMEM((heads, chunk, lanes), F32)],
                name="attend",
        compiler_params=vmem(14),
                cost_estimate=cost(4 * chunk * prefix_rows * heads * lanes, chunk * prefix_rows * heads, 8_000_000),
            )(flag, q, acc, peaks, prefix)
        )
    out = None
    for c in range(CHUNKS):
        far = across(attended[c], 2)
        core = across(attended[c], 1)
        both = across(attended[c], 3)
        operands = [lengths, rank, attended[c], core, far, both, w_out, w_core, w_far, w_both, rows, step_rates.reshape(1, width)]
        specs = [SMEM] * 2 + [VMEM] * 8 + [pl.BlockSpec((chunk, width), lambda i, c=c: (c, 0)), VMEM]
        aliases = {}
        if out is not None:
            aliases = {len(operands): 0}
            operands.append(out)
            specs.append(ANY)
        out = pl.pallas_call(
            lambda *refs, c=c: output_kernel(*refs, tile=256, start=c * chunk),
            grid=(1,),
            out_shape=shaped((part, suf), BF16),
            in_specs=specs,
            out_specs=pl.BlockSpec((part, chunk), lambda i, c=c: (0, c)),
            input_output_aliases=aliases,
            scratch_shapes=[pltpu.VMEM((chunk, width), F32)],
            name="output",
        compiler_params=vmem(20),
            cost_estimate=cost(2 * chunk * width * width, 0, 6_000_000),
        )(*operands)
    return out.T.reshape(1, suf, part)


def solution(mesh):
    in_specs = (
        P("req", None, None),
        P("req"),
        P("req"),
        P(),
        P("req", "tp", None),
        P(None, "tp"),
        P(None, "tp"),
        P(None, "tp"),
        P("tp", None),
        P("tp", None),
        P(),
    )
    out_specs = P("req", None, "tp")
    return jax.shard_map(local, mesh=mesh, in_specs=in_specs, out_specs=out_specs, check_vma=False)
```

profile of v0, /device:TPU:1, one launch (start us, length us, event | category | flops | bytes accessed | tf_op | source)
XLA Modules:
  0.0 123.6 jit_solution(13518504926248005268)
XLA Ops:
  2.9 2.1 %collective-permute-start.7 = (bf16[6,64,128]{2,1,0:T(8,128)(2,1)S(1)}, bf16[6,64,128]{2,1,0:T(8,128)(2,1)S(1)}, u32[]{:S(2)}, u32[]{:S(2)}) collective-permute-start(bf16[6,64,128]{2,1,0:T(8,128)(2,1)S(1)} %get-tuple-element.133.a_ref), channel_id=1, source_target_pairs={{128,0},{132,4},{136,8},{140,12},{144,16},{148,20},{152,24},{156,2... | collective-permute-start | bytes 294920 | tf_op jit(solution)/shard_map/ppermute | solution.py:34
  5.0 6.9 %collective-permute-start.8 = (bf16[6,64,128]{2,1,0:T(8,128)(2,1)S(1)}, bf16[6,64,128]{2,1,0:T(8,128)(2,1)S(1)}, u32[]{:S(2)}, u32[]{:S(2)}) collective-permute-start(bf16[6,64,128]{2,1,0:T(8,128)(2,1)S(1)} %get-tuple-element.133.a_ref), channel_id=1, source_target_pairs={{64,0},{68,4},{72,8},{76,12},{80,16},{84,20},{88,24},{92,28},{96,3... | collective-permute-start | bytes 294920 | tf_op jit(solution)/shard_map/ppermute | solution.py:34
  11.9 2.1 %collective-permute-done.8.c_ref = bf16[6,64,128]{2,1,0:T(8,128)(2,1)S(1)} collective-permute-done((bf16[6,64,128]{2,1,0:T(8,128)(2,1)S(1)}, bf16[6,64,128]{2,1,0:T(8,128)(2,1)S(1)}, u32[]{:S(2)}, u32[]{:S(2)}) %collective-permute-start.8) | collective-permute-done | bytes 98336 | tf_op jit(solution)/shard_map/ppermute | solution.py:34
  14.0 6.5 %collective-permute-done.9.d_ref = bf16[6,64,128]{2,1,0:T(8,128)(2,1)S(1)} collective-permute-done((bf16[6,64,128]{2,1,0:T(8,128)(2,1)S(1)}, bf16[6,64,128]{2,1,0:T(8,128)(2,1)S(1)}, u32[]{:S(2)}, u32[]{:S(2)}) %collective-permute-start.9) | collective-permute-done | bytes 98336 | tf_op jit(solution)/shard_map/ppermute | solution.py:34
  20.5 1.3 %collective-permute-start.10 = (bf16[4,6,32,128]{3,2,1,0:T(8,128)(2,1)S(1)}, bf16[4,6,32,128]{3,2,1,0:T(8,128)(2,1)S(1)}, u32[]{:S(2)}, u32[]{:S(2)}) collective-permute-start(bf16[4,6,32,128]{3,2,1,0:T(8,128)(2,1)S(1)} %get-tuple-element.134.refs_2_), channel_id=1, source_target_pairs={{16,0},{20,4},{24,8},{28,12},{32,16},{36,20},{40,24},{44,28},{48,3... | collective-permute-start | bytes 589832 | tf_op jit(solution)/shard_map/ppermute | solution.py:34
  23.6 3.5 %collective-permute-start.13 = (bf16[4,6,32,128]{3,2,1,0:T(8,128)(2,1)S(1)}, bf16[4,6,32,128]{3,2,1,0:T(8,128)(2,1)S(1)}, u32[]{:S(2)}, u32[]{:S(2)}) collective-permute-start(bf16[4,6,32,128]{3,2,1,0:T(8,128)(2,1)S(1)} %get-tuple-element.135.refs_6_), channel_id=1, source_target_pairs={{4,0},{8,4},{12,8},{0,12},{20,16},{24,20},{28,24},{16,28},{36,32},... | collective-permute-start | bytes 589832 | tf_op jit(solution)/shard_map/ppermute | solution.py:34
  27.1 2.9 %collective-permute-start.15 = (bf16[4,6,32,128]{3,2,1,0:T(8,128)(2,1)S(1)}, bf16[4,6,32,128]{3,2,1,0:T(8,128)(2,1)S(1)}, u32[]{:S(2)}, u32[]{:S(2)}) collective-permute-start(bf16[4,6,32,128]{3,2,1,0:T(8,128)(2,1)S(1)} %get-tuple-element.135.refs_6_), channel_id=1, source_target_pairs={{8,0},{12,4},{0,8},{4,12},{24,16},{28,20},{16,24},{20,28},{40,32},... | collective-permute-start | bytes 589832 | tf_op jit(solution)/shard_map/ppermute | solution.py:34
  31.3 2.8 %plan.1 = (s32[128]{0:T(128)S(1)}, s32[32]{0:T(128)S(1)}, s32[1]{0:T(128)}) custom-call(s32[1]{0:T(128)S(6)} %copy.17.member_ref.refs_0_, s32[1]{0:T(128)} %bitcast.6.place_ref, s32[4,16]{1,0:T(4,128)S(1)} %copy-done.9, s32[128]{0:T(128)S(1)} %copy-done.10), custom_call_target="tpu_custom_call" | custom-call | bytes 1000000 | tf_op jit(solution)/shard_map/plan/pallas_call | solution.py:410
  35.7 1.6 %pack.3 = (bf16[16,5,32,128]{3,2,1,0:T(8,128)(2,1)S(1)}, bf16[8,5,32,128]{3,2,1,0:T(8,128)(2,1)S(1)}, bf16[8,5,32,128]{3,2,1,0:T(8,128)(2,1)S(1)}, bf16[8,5,32,1...) custom-call(s32[1]{0:T(128)S(6)} %copy.17.member_ref.refs_0_, ...), custom_call_target="tpu_custom_call" | custom-call | bytes 4000000 | tf_op jit(solution)/shard_map/pack/pallas_call | solution.py:442
  37.3 2.8 %collective-permute-start.21 = (bf16[4,5,32,128]{3,2,1,0:T(8,128)(2,1)S(1)}, bf16[4,5,32,128]{3,2,1,0:T(8,128)(2,1)S(1)}, u32[]{:S(2)}, u32[]{:S(2)}) collective-permute-start(bf16[4,5,32,128]{3,2,1,0:T(8,128)(2,1)S(1)} %get-tuple-element.143), channel_id=1, source_target_pairs={{32,0},{36,4},{40,8},{44,12},{48,16},{52,20},{56,24},{60,28},{64,3... | collective-permute-start | bytes 491528 | tf_op jit(solution)/shard_map/ppermute | solution.py:34
  40.1 1.8 %collective-permute-start.16 = (bf16[8,5,32,128]{3,2,1,0:T(8,128)(2,1)S(1)}, bf16[8,5,32,128]{3,2,1,0:T(8,128)(2,1)S(1)}, u32[]{:S(2)}, u32[]{:S(2)}) collective-permute-start(bf16[8,5,32,128]{3,2,1,0:T(8,128)(2,1)S(1)} %get-tuple-element.137), channel_id=1, source_target_pairs={{4,0},{8,4},{12,8},{0,12},{20,16},{24,20},{28,24},{16,28},{36,32},... | collective-permute-start | bytes 983048 | tf_op jit(solution)/shard_map/ppermute | solution.py:34
  41.9 2.0 %collective-permute-start.18 = (bf16[8,5,32,128]{3,2,1,0:T(8,128)(2,1)S(1)}, bf16[8,5,32,128]{3,2,1,0:T(8,128)(2,1)S(1)}, u32[]{:S(2)}, u32[]{:S(2)}) collective-permute-start(bf16[8,5,32,128]{3,2,1,0:T(8,128)(2,1)S(1)} %get-tuple-element.139), channel_id=1, source_target_pairs={{8,0},{12,4},{0,8},{4,12},{24,16},{28,20},{16,24},{20,28},{40,32},... | collective-permute-start | bytes 983048 | tf_op jit(solution)/shard_map/ppermute | solution.py:34
  44.3 3.3 %collective-permute-start.19 = (bf16[8,5,32,128]{3,2,1,0:T(8,128)(2,1)S(1)}, bf16[8,5,32,128]{3,2,1,0:T(8,128)(2,1)S(1)}, u32[]{:S(2)}, u32[]{:S(2)}) collective-permute-start(bf16[8,5,32,128]{3,2,1,0:T(8,128)(2,1)S(1)} %get-tuple-element.141), channel_id=1, source_target_pairs={{16,0},{20,4},{24,8},{28,12},{32,16},{36,20},{40,24},{44,28},{48,3... | collective-permute-start | bytes 983048 | tf_op jit(solution)/shard_map/ppermute | solution.py:34
  47.6 1.8 %collective-permute-start.20 = (bf16[8,5,32,128]{3,2,1,0:T(8,128)(2,1)S(1)}, bf16[8,5,32,128]{3,2,1,0:T(8,128)(2,1)S(1)}, u32[]{:S(2)}, u32[]{:S(2)}) collective-permute-start(bf16[8,5,32,128]{3,2,1,0:T(8,128)(2,1)S(1)} %get-tuple-element.142), channel_id=1, source_target_pairs={{112,0},{116,4},{120,8},{124,12},{0,16},{4,20},{8,24},{12,28},{16,... | collective-permute-start | bytes 983048 | tf_op jit(solution)/shard_map/ppermute | solution.py:34
  50.0 1.2 collective-permute-done.17
  51.2 3.1 %collective-permute-done.18 = bf16[8,5,32,128]{3,2,1,0:T(8,128)(2,1)S(1)} collective-permute-done((bf16[8,5,32,128]{3,2,1,0:T(8,128)(2,1)S(1)}, bf16[8,5,32,128]{3,2,1,0:T(8,128)(2,1)S(1)}, u32[]{:S(2)}, u32[]{:S(2)}) %collective-permute-start.18) | collective-permute-done | bytes 327712 | tf_op jit(solution)/shard_map/ppermute | solution.py:34
  54.4 1.6 %collective-permute-done.20 = bf16[8,5,32,128]{3,2,1,0:T(8,128)(2,1)S(1)} collective-permute-done((bf16[8,5,32,128]{3,2,1,0:T(8,128)(2,1)S(1)}, bf16[8,5,32,128]{3,2,1,0:T(8,128)(2,1)S(1)}, u32[]{:S(2)}, u32[]{:S(2)}) %collective-permute-start.20) | collective-permute-done | bytes 327712 | tf_op jit(solution)/shard_map/ppermute | solution.py:34
  56.1 2.6 %conditional.1 = (bf16[5,1024,128]{2,1,0:T(8,128)(2,1)S(1)}) conditional(s32[]{:T(128)} %bitcast.7, (s32[32]{0:T(128)S(1)}, bf16[16,5,32,128]{3,2,1,0:T(8,128)(2,1)S(1)}, bf16[8,5,32,128]{3,2,1,0:T(8,128)(2,1)S(1)}, bf16[8,5,32,128]{3,2,1,0:T(8,128)(2,1)S(1)}, bf16[8,5,32,128]{3,2,1,0:T(8,128)(2,1)S(1)}, ...), branch_computations={%region_0.0_spmd, %region_1.0_spmd} | conditional | bytes 14864608 | solution.py:467
  56.1 2.4 %select.2 = bf16[5,1024,128]{2,1,0:T(8,128)(2,1)S(1)} custom-call(s32[32]{0:T(128)S(1)} %get-tuple-element.68.recv_ref, bf16[16,5,32,128]{3,2,1,0:T(8,128)(2,1)S(1)} %get-tuple-element.69.rest_0_, bf16[8,5,32,128]{3,2,1,0:T(8,128)(2,1)S(1)} %get-tuple-element.70.rest_1_, bf16[8,5,32,128]{3,2,1,0:T(8,128)(2,1)S(1)} %get-tuple-element.71.rest_2_, ...), custom_call_target="tpu_custom_call" | custom-call | bytes 3000000 | tf_op jit(solution)/shard_map/cond/branch_0_fun/select/pallas_call | solution.py:455
  59.8 2.4 %collective-permute-start.27 = (bf16[320,1280]{1,0:T(8,128)(2,1)S(1)}, bf16[320,1280]{1,0:T(8,128)(2,1)S(1)}, u32[]{:S(2)}, u32[]{:S(2)}) collective-permute-start(bf16[320,1280]{1,0:T(8,128)(2,1)S(1)} %copy-done.1), channel_id=1, source_target_pairs={{0,2},{1,3},{2,0},{3,1},{4,6},{5,7},{6,4},{7,5},{8,10},{9,11},{10,... | collective-permute-start | bytes 2457608 | tf_op jit(solution)/shard_map/ppermute | solution.py:390
  62.2 6.5 %collective-permute-start.26 = (bf16[320,1280]{1,0:T(8,128)(2,1)S(1)}, bf16[320,1280]{1,0:T(8,128)(2,1)}, u32[]{:S(2)}, u32[]{:S(2)}) collective-permute-start(bf16[320,1280]{1,0:T(8,128)(2,1)S(1)} %copy-done.1), channel_id=1, source_target_pairs={{0,1},{1,0},{2,3},{3,2},{4,5},{5,4},{6,7},{7,6},{8,9},{9,8},{10,11... | collective-permute-start | bytes 2457608 | tf_op jit(solution)/shard_map/ppermute | solution.py:390
  68.7 6.4 %collective-permute-done.27.refs_8_ = bf16[320,1280]{1,0:T(8,128)(2,1)S(1)} collective-permute-done((bf16[320,1280]{1,0:T(8,128)(2,1)S(1)}, bf16[320,1280]{1,0:T(8,128)(2,1)S(1)}, u32[]{:S(2)}, u32[]{:S(2)}) %collective-permute-start.27) | collective-permute-done | bytes 819232 | tf_op jit(solution)/shard_map/ppermute | solution.py:390
  75.1 6.9 %collective-permute-start.28 = (bf16[320,1280]{1,0:T(8,128)(2,1)S(1)}, bf16[320,1280]{1,0:T(8,128)(2,1)}, u32[]{:S(2)}, u32[]{:S(2)}) collective-permute-start(bf16[320,1280]{1,0:T(8,128)(2,1)S(1)} %collective-permute-done.27.refs_8_), channel_id=1, source_target_pairs={{0,1},{1,0},{2,3},{3,2},{4,5},{5,4},{6,7},{7,6},{8,9},{9,8},{10,11... | collective-permute-start | bytes 2457608 | tf_op jit(solution)/shard_map/ppermute | solution.py:390
  86.1 2.0 %qkv.1 = (bf16[5,512,128]{2,1,0:T(8,128)(2,1)S(1)}, bf16[5,512,128]{2,1,0:T(8,128)(2,1)S(1)}) custom-call(bf16[512,1280]{1,0:T(8,128)(2,1)S(1)} %bitcast.11, bf16[320,1280]{1,0:T(8,128)(2,1)S(1)} %bitcast.15, bf16[320,1280]{1,0:T(8,128)(2,1)S(1)} %bitcast.16, bf16[320,1280]{1,0:T(8,128)(2,1)S(1)} %bitcast.17, f32[5,64]{1,0:T(8,128)S(1)} %copy-done.8), custom_call_target="tpu_custom_call" | custom-call | flops 1258291200 | bytes 10000000 | tf_op jit(solution)/shard_map/qkv/pallas_call | solution.py:504
  88.1 4.5 %suffix.1 = (f32[5,512,128]{2,1,0:T(8,128)S(1)}, f32[512,128]{1,0:T(8,128)S(1)}) custom-call(s32[1]{0:T(128)S(6)} %copy.18.refs_0_, s32[1]{0:T(128)} %get-tuple-element.125.refs_1_.refs_0_, bf16[5,512,128]{2,1,0:T(8,128)(2,1)S(1)} %get-tuple-element.126.refs_2_.refs_1_, bf16[5,512,128]{2,1,0:T(8,128)(2,1)S(1)} %get-tuple-element.127.refs_3_), custom_call_target="tpu_custom_call" | custom-call | flops 671088640 | bytes 10000000 | tf_op jit(solution)/shard_map/suffix/pallas_call | solution.py:514
  92.6 4.2 %attend.3.refs_2_ = bf16[256,320]{1,0:T(8,128)(2,1)S(1)} custom-call(s32[1]{0:T(128)} %get-tuple-element.125.refs_1_.refs_0_, bf16[5,512,128]{2,1,0:T(8,128)(2,1)S(1)} %get-tuple-element.126.refs_2_.refs_1_, f32[5,512,128]{2,1,0:T(8,128)S(1)} %get-tuple-element.128.refs_2_, f32[512,128]{1,0:T(8,128)S(1)} %get-tuple-element.129.refs_3_, ...), custom_call_target="tpu_custom_call" | custom-call | flops 671088640 | bytes 8000000 | tf_op jit(solution)/shard_map/attend/pallas_call | solution.py:532
  96.9 2.5 %collective-permute-start.30 = (bf16[256,320]{1,0:T(8,128)(2,1)S(1)}, bf16[256,320]{1,0:T(8,128)(2,1)S(1)}, u32[]{:S(2)}, u32[]{:S(2)}) collective-permute-start(bf16[256,320]{1,0:T(8,128)(2,1)S(1)} %attend.3.refs_2_), channel_id=1, source_target_pairs={{0,2},{1,3},{2,0},{3,1},{4,6},{5,7},{6,4},{7,5},{8,10},{9,11},{10,... | collective-permute-start | bytes 491528 | tf_op jit(solution)/shard_map/ppermute | solution.py:390
  100.6 4.4 %attend.2.refs_2_ = bf16[256,320]{1,0:T(8,128)(2,1)S(1)} custom-call(s32[1]{0:T(128)} %get-tuple-element.125.refs_1_.refs_0_, bf16[5,512,128]{2,1,0:T(8,128)(2,1)S(1)} %get-tuple-element.126.refs_2_.refs_1_, f32[5,512,128]{2,1,0:T(8,128)S(1)} %get-tuple-element.128.refs_2_, f32[512,128]{1,0:T(8,128)S(1)} %get-tuple-element.129.refs_3_, ...), custom_call_target="tpu_custom_call" | custom-call | flops 671088640 | bytes 8000000 | tf_op jit(solution)/shard_map/attend/pallas_call | solution.py:532
  105.8 2.4 %collective-permute-start.24 = (bf16[256,320]{1,0:T(8,128)(2,1)S(1)}, bf16[256,320]{1,0:T(8,128)(2,1)}, u32[]{:S(2)}, u32[]{:S(2)}) collective-permute-start(bf16[256,320]{1,0:T(8,128)(2,1)S(1)} %attend.2.refs_2_), channel_id=1, source_target_pairs={{0,2},{1,3},{2,0},{3,1},{4,6},{5,7},{6,4},{7,5},{8,10},{9,11},{10,... | collective-permute-start | bytes 491528 | tf_op jit(solution)/shard_map/ppermute | solution.py:390
  110.1 2.1 %collective-permute-start.25 = (bf16[256,320]{1,0:T(8,128)(2,1)S(1)}, bf16[256,320]{1,0:T(8,128)(2,1)}, u32[]{:S(2)}, u32[]{:S(2)}) collective-permute-start(bf16[256,320]{1,0:T(8,128)(2,1)S(1)} %attend.2.refs_2_), channel_id=1, source_target_pairs={{0,3},{1,2},{2,1},{3,0},{4,7},{5,6},{6,5},{7,4},{8,11},{9,10},{10,... | collective-permute-start | bytes 491528 | tf_op jit(solution)/shard_map/ppermute | solution.py:390
  114.0 4.2 %output.2.refs_12_ = bf16[320,512]{1,0:T(8,128)(2,1)} custom-call(s32[1]{0:T(128)S(6)} %copy.18.refs_0_, s32[1]{0:T(128)} %bitcast.refs_1_, bf16[256,320]{1,0:T(8,128)(2,1)S(1)} %attend.3.refs_2_, bf16[256,320]{1,0:T(8,128)(2,1)S(1)} %collective-permute-done.29.refs_3_, bf16[256,320]{1,0:T(8,128)(2,1)S(1)} %copy-done.3, bf16[256,320]{1,0:T(8,128)(2,1)S(1)} %copy-done.5, ...), custom_call_target="tpu_custom_call" | custom-call | flops 838860800 | bytes 6000000 | tf_op jit(solution)/shard_map/output/pallas_call | solution.py:562
  119.1 4.4 %output.3 = bf16[320,512]{1,0:T(8,128)(2,1)} custom-call(s32[1]{0:T(128)S(6)} %copy.18.refs_0_, s32[1]{0:T(128)} %bitcast.refs_1_, bf16[256,320]{1,0:T(8,128)(2,1)S(1)} %attend.2.refs_2_, bf16[256,320]{1,0:T(8,128)(2,1)} %collective-permute-done.23.refs_3_, bf16[256,320]{1,0:T(8,128)(2,1)} %collective-permute-done.24.refs_4_, ...), custom_call_target="tpu_custom_call", output_to_operand_aliasing={{}: (12, {})} | custom-call | flops 838860800 | bytes 6000000 | tf_op jit(solution)/shard_map/output/pallas_call | solution.py:562
  (81 shorter events, 18.5 us)
Async XLA Ops:
  2.9 9.0 %collective-permute-start.7 = (bf16[6,64,128]{2,1,0:T(8,128)(2,1)S(1)}, bf16[6,64,128]{2,1,0:T(8,128)(2,1)S(1)}, u32[]{:S(2)}, u32[]{:S(2)}) collective-permute-start(bf16[6,64,128]{2,1,0:T(8,128)(2,1)S(1)} %get-tuple-element.133.a_ref), channel_id=1, source_target_pairs={{128,0},{132,4},{136,8},{140,12},{144,16},{148,20},{152,24},{156,2... | collective-permute-start | bytes 294920 | tf_op jit(solution)/shard_map/ppermute | solution.py:34
  5.0 9.0 %collective-permute-start.8 = (bf16[6,64,128]{2,1,0:T(8,128)(2,1)S(1)}, bf16[6,64,128]{2,1,0:T(8,128)(2,1)S(1)}, u32[]{:S(2)}, u32[]{:S(2)}) collective-permute-start(bf16[6,64,128]{2,1,0:T(8,128)(2,1)S(1)} %get-tuple-element.133.a_ref), channel_id=1, source_target_pairs={{64,0},{68,4},{72,8},{76,12},{80,16},{84,20},{88,24},{92,28},{96,3... | collective-permute-start | bytes 294920 | tf_op jit(solution)/shard_map/ppermute | solution.py:34
  11.9 8.6 %collective-permute-start.9 = (bf16[6,64,128]{2,1,0:T(8,128)(2,1)S(1)}, bf16[6,64,128]{2,1,0:T(8,128)(2,1)S(1)}, u32[]{:S(2)}, u32[]{:S(2)}) collective-permute-start(bf16[6,64,128]{2,1,0:T(8,128)(2,1)S(1)} %get-tuple-element.133.a_ref), channel_id=1, source_target_pairs={{192,0},{196,4},{200,8},{204,12},{208,16},{212,20},{216,24},{220,2... | collective-permute-start | bytes 294920 | tf_op jit(solution)/shard_map/ppermute | solution.py:34
  20.5 35.5 %copy-start.16 = (bf16[4,6,32,128]{3,2,1,0:T(8,128)(2,1)}, bf16[4,6,32,128]{3,2,1,0:T(8,128)(2,1)S(1)}, u32[]{:S(2)}) copy-start(bf16[4,6,32,128]{3,2,1,0:T(8,128)(2,1)S(1)} %get-tuple-element.134.refs_2_) | copy-start | bytes 589828
  20.5 35.5 %copy-start.17 = (bf16[4,6,32,128]{3,2,1,0:T(8,128)(2,1)}, bf16[4,6,32,128]{3,2,1,0:T(8,128)(2,1)S(1)}, u32[]{:S(2)}) copy-start(bf16[4,6,32,128]{3,2,1,0:T(8,128)(2,1)S(1)} %get-tuple-element.135.refs_6_) | copy-start | bytes 589828
  20.5 6.6 %collective-permute-start.10 = (bf16[4,6,32,128]{3,2,1,0:T(8,128)(2,1)S(1)}, bf16[4,6,32,128]{3,2,1,0:T(8,128)(2,1)S(1)}, u32[]{:S(2)}, u32[]{:S(2)}) collective-permute-start(bf16[4,6,32,128]{3,2,1,0:T(8,128)(2,1)S(1)} %get-tuple-element.134.refs_2_), channel_id=1, source_target_pairs={{16,0},{20,4},{24,8},{28,12},{32,16},{36,20},{40,24},{44,28},{48,3... | collective-permute-start | bytes 589832 | tf_op jit(solution)/shard_map/ppermute | solution.py:34
  21.8 12.3 %collective-permute-start.11 = (bf16[4,6,32,128]{3,2,1,0:T(8,128)(2,1)S(1)}, bf16[4,6,32,128]{3,2,1,0:T(8,128)(2,1)S(1)}, u32[]{:S(2)}, u32[]{:S(2)}) collective-permute-start(bf16[4,6,32,128]{3,2,1,0:T(8,128)(2,1)S(1)} %get-tuple-element.134.refs_2_), channel_id=1, source_target_pairs={{112,0},{116,4},{120,8},{124,12},{0,16},{4,20},{8,24},{12,28},{16,... | collective-permute-start | bytes 589832 | tf_op jit(solution)/shard_map/ppermute | solution.py:34
  22.5 12.2 %collective-permute-start.12 = (bf16[4,6,32,128]{3,2,1,0:T(8,128)(2,1)S(1)}, bf16[4,6,32,128]{3,2,1,0:T(8,128)(2,1)S(1)}, u32[]{:S(2)}, u32[]{:S(2)}) collective-permute-start(bf16[4,6,32,128]{3,2,1,0:T(8,128)(2,1)S(1)} %get-tuple-element.134.refs_2_), channel_id=1, source_target_pairs={{96,0},{100,4},{104,8},{108,12},{112,16},{116,20},{120,24},{124,28... | collective-permute-start | bytes 589832 | tf_op jit(solution)/shard_map/ppermute | solution.py:34
  23.6 11.1 %collective-permute-start.13 = (bf16[4,6,32,128]{3,2,1,0:T(8,128)(2,1)S(1)}, bf16[4,6,32,128]{3,2,1,0:T(8,128)(2,1)S(1)}, u32[]{:S(2)}, u32[]{:S(2)}) collective-permute-start(bf16[4,6,32,128]{3,2,1,0:T(8,128)(2,1)S(1)} %get-tuple-element.135.refs_6_), channel_id=1, source_target_pairs={{4,0},{8,4},{12,8},{0,12},{20,16},{24,20},{28,24},{16,28},{36,32},... | collective-permute-start | bytes 589832 | tf_op jit(solution)/shard_map/ppermute | solution.py:34
  27.1 8.6 %collective-permute-start.14 = (bf16[4,6,32,128]{3,2,1,0:T(8,128)(2,1)S(1)}, bf16[4,6,32,128]{3,2,1,0:T(8,128)(2,1)S(1)}, u32[]{:S(2)}, u32[]{:S(2)}) collective-permute-start(bf16[4,6,32,128]{3,2,1,0:T(8,128)(2,1)S(1)} %get-tuple-element.135.refs_6_), channel_id=1, source_target_pairs={{12,0},{0,4},{4,8},{8,12},{28,16},{16,20},{20,24},{24,28},{44,32},... | collective-permute-start | bytes 589832 | tf_op jit(solution)/shard_map/ppermute | solution.py:34
  27.1 28.9 %copy-start.18 = (bf16[4,6,32,128]{3,2,1,0:T(8,128)(2,1)}, bf16[4,6,32,128]{3,2,1,0:T(8,128)(2,1)S(1)}, u32[]{:S(2)}) copy-start(bf16[4,6,32,128]{3,2,1,0:T(8,128)(2,1)S(1)} %collective-permute-done.10.refs_3_) | copy-start | bytes 589828
  27.1 8.6 %collective-permute-start.15 = (bf16[4,6,32,128]{3,2,1,0:T(8,128)(2,1)S(1)}, bf16[4,6,32,128]{3,2,1,0:T(8,128)(2,1)S(1)}, u32[]{:S(2)}, u32[]{:S(2)}) collective-permute-start(bf16[4,6,32,128]{3,2,1,0:T(8,128)(2,1)S(1)} %get-tuple-element.135.refs_6_), channel_id=1, source_target_pairs={{8,0},{12,4},{0,8},{4,12},{24,16},{28,20},{16,24},{20,28},{40,32},... | collective-permute-start | bytes 589832 | tf_op jit(solution)/shard_map/ppermute | solution.py:34
  34.1 21.9 %copy-start.19 = (bf16[4,6,32,128]{3,2,1,0:T(8,128)(2,1)}, bf16[4,6,32,128]{3,2,1,0:T(8,128)(2,1)S(1)}, u32[]{:S(2)}) copy-start(bf16[4,6,32,128]{3,2,1,0:T(8,128)(2,1)S(1)} %collective-permute-done.11.refs_4_) | copy-start | bytes 589828
  34.7 21.3 %copy-start.21 = (bf16[4,6,32,128]{3,2,1,0:T(8,128)(2,1)}, bf16[4,6,32,128]{3,2,1,0:T(8,128)(2,1)S(1)}, u32[]{:S(2)}) copy-start(bf16[4,6,32,128]{3,2,1,0:T(8,128)(2,1)S(1)} %collective-permute-done.13.refs_7_) | copy-start | bytes 589828
  37.3 7.0 %collective-permute-start.21 = (bf16[4,5,32,128]{3,2,1,0:T(8,128)(2,1)S(1)}, bf16[4,5,32,128]{3,2,1,0:T(8,128)(2,1)S(1)}, u32[]{:S(2)}, u32[]{:S(2)}) collective-permute-start(bf16[4,5,32,128]{3,2,1,0:T(8,128)(2,1)S(1)} %get-tuple-element.143), channel_id=1, source_target_pairs={{32,0},{36,4},{40,8},{44,12},{48,16},{52,20},{56,24},{60,28},{64,3... | collective-permute-start | bytes 491528 | tf_op jit(solution)/shard_map/ppermute | solution.py:34
  40.1 7.5 %collective-permute-start.22 = (bf16[4,5,32,128]{3,2,1,0:T(8,128)(2,1)S(1)}, bf16[4,5,32,128]{3,2,1,0:T(8,128)(2,1)S(1)}, u32[]{:S(2)}, u32[]{:S(2)}) collective-permute-start(bf16[4,5,32,128]{3,2,1,0:T(8,128)(2,1)S(1)} %get-tuple-element.144), channel_id=1, source_target_pairs={{96,0},{100,4},{104,8},{108,12},{112,16},{116,20},{120,24},{124,28... | collective-permute-start | bytes 491528 | tf_op jit(solution)/shard_map/ppermute | solution.py:34
  40.1 9.9 %collective-permute-start.16 = (bf16[8,5,32,128]{3,2,1,0:T(8,128)(2,1)S(1)}, bf16[8,5,32,128]{3,2,1,0:T(8,128)(2,1)S(1)}, u32[]{:S(2)}, u32[]{:S(2)}) collective-permute-start(bf16[8,5,32,128]{3,2,1,0:T(8,128)(2,1)S(1)} %get-tuple-element.137), channel_id=1, source_target_pairs={{4,0},{8,4},{12,8},{0,12},{20,16},{24,20},{28,24},{16,28},{36,32},... | collective-permute-start | bytes 983048 | tf_op jit(solution)/shard_map/ppermute | solution.py:34
  41.9 9.4 %collective-permute-start.17 = (bf16[8,5,32,128]{3,2,1,0:T(8,128)(2,1)S(1)}, bf16[8,5,32,128]{3,2,1,0:T(8,128)(2,1)S(1)}, u32[]{:S(2)}, u32[]{:S(2)}) collective-permute-start(bf16[8,5,32,128]{3,2,1,0:T(8,128)(2,1)S(1)} %get-tuple-element.138), channel_id=1, source_target_pairs={{12,0},{0,4},{4,8},{8,12},{28,16},{16,20},{20,24},{24,28},{44,32},... | collective-permute-start | bytes 983048 | tf_op jit(solution)/shard_map/ppermute | solution.py:34
  41.9 12.5 %collective-permute-start.18 = (bf16[8,5,32,128]{3,2,1,0:T(8,128)(2,1)S(1)}, bf16[8,5,32,128]{3,2,1,0:T(8,128)(2,1)S(1)}, u32[]{:S(2)}, u32[]{:S(2)}) collective-permute-start(bf16[8,5,32,128]{3,2,1,0:T(8,128)(2,1)S(1)} %get-tuple-element.139), channel_id=1, source_target_pairs={{8,0},{12,4},{0,8},{4,12},{24,16},{28,20},{16,24},{20,28},{40,32},... | collective-permute-start | bytes 983048 | tf_op jit(solution)/shard_map/ppermute | solution.py:34
  44.3 10.1 %collective-permute-start.19 = (bf16[8,5,32,128]{3,2,1,0:T(8,128)(2,1)S(1)}, bf16[8,5,32,128]{3,2,1,0:T(8,128)(2,1)S(1)}, u32[]{:S(2)}, u32[]{:S(2)}) collective-permute-start(bf16[8,5,32,128]{3,2,1,0:T(8,128)(2,1)S(1)} %get-tuple-element.141), channel_id=1, source_target_pairs={{16,0},{20,4},{24,8},{28,12},{32,16},{36,20},{40,24},{44,28},{48,3... | collective-permute-start | bytes 983048 | tf_op jit(solution)/shard_map/ppermute | solution.py:34
  47.6 8.4 %collective-permute-start.20 = (bf16[8,5,32,128]{3,2,1,0:T(8,128)(2,1)S(1)}, bf16[8,5,32,128]{3,2,1,0:T(8,128)(2,1)S(1)}, u32[]{:S(2)}, u32[]{:S(2)}) collective-permute-start(bf16[8,5,32,128]{3,2,1,0:T(8,128)(2,1)S(1)} %get-tuple-element.142), channel_id=1, source_target_pairs={{112,0},{116,4},{120,8},{124,12},{0,16},{4,20},{8,24},{12,28},{16,... | collective-permute-start | bytes 983048 | tf_op jit(solution)/shard_map/ppermute | solution.py:34
  56.1 26.6 %copy-start = (bf16[1,512,1280]{2,1,0:T(8,128)(2,1)S(1)}, bf16[1,512,1280]{2,1,0:T(8,128)(2,1)}, u32[]{:S(2)}) copy-start(bf16[1,512,1280]{2,1,0:T(8,128)(2,1)} %param.14) | copy-start | bytes 3932164
  56.1 26.5 %copy-start.8 = (f32[5,64]{1,0:T(8,128)S(1)}, f32[5,64]{1,0:T(8,128)}, u32[]{:S(2)}) copy-start(f32[5,64]{1,0:T(8,128)} %refs_4_.1) | copy-start | bytes 3844
  59.8 15.3 %collective-permute-start.27 = (bf16[320,1280]{1,0:T(8,128)(2,1)S(1)}, bf16[320,1280]{1,0:T(8,128)(2,1)S(1)}, u32[]{:S(2)}, u32[]{:S(2)}) collective-permute-start(bf16[320,1280]{1,0:T(8,128)(2,1)S(1)} %copy-done.1), channel_id=1, source_target_pairs={{0,2},{1,3},{2,0},{3,1},{4,6},{5,7},{6,4},{7,5},{8,10},{9,11},{10,... | collective-permute-start | bytes 2457608 | tf_op jit(solution)/shard_map/ppermute | solution.py:390
  62.2 50.0 %collective-permute-start.26 = (bf16[320,1280]{1,0:T(8,128)(2,1)S(1)}, bf16[320,1280]{1,0:T(8,128)(2,1)}, u32[]{:S(2)}, u32[]{:S(2)}) collective-permute-start(bf16[320,1280]{1,0:T(8,128)(2,1)S(1)} %copy-done.1), channel_id=1, source_target_pairs={{0,1},{1,0},{2,3},{3,2},{4,5},{5,4},{6,7},{7,6},{8,9},{9,8},{10,11... | collective-permute-start | bytes 2457608 | tf_op jit(solution)/shard_map/ppermute | solution.py:390
  75.1 37.1 %collective-permute-start.28 = (bf16[320,1280]{1,0:T(8,128)(2,1)S(1)}, bf16[320,1280]{1,0:T(8,128)(2,1)}, u32[]{:S(2)}, u32[]{:S(2)}) collective-permute-start(bf16[320,1280]{1,0:T(8,128)(2,1)S(1)} %collective-permute-done.27.refs_8_), channel_id=1, source_target_pairs={{0,1},{1,0},{2,3},{3,2},{4,5},{5,4},{6,7},{7,6},{8,9},{9,8},{10,11... | collective-permute-start | bytes 2457608 | tf_op jit(solution)/shard_map/ppermute | solution.py:390
  96.8 8.2 %collective-permute-start.29 = (bf16[256,320]{1,0:T(8,128)(2,1)S(1)}, bf16[256,320]{1,0:T(8,128)(2,1)S(1)}, u32[]{:S(2)}, u32[]{:S(2)}) collective-permute-start(bf16[256,320]{1,0:T(8,128)(2,1)S(1)} %attend.3.refs_2_), channel_id=1, source_target_pairs={{0,1},{1,0},{2,3},{3,2},{4,5},{5,4},{6,7},{7,6},{8,9},{9,8},{10,11... | collective-permute-start | bytes 491528 | tf_op jit(solution)/shard_map/ppermute | solution.py:390
  96.9 8.2 %collective-permute-start.30 = (bf16[256,320]{1,0:T(8,128)(2,1)S(1)}, bf16[256,320]{1,0:T(8,128)(2,1)S(1)}, u32[]{:S(2)}, u32[]{:S(2)}) collective-permute-start(bf16[256,320]{1,0:T(8,128)(2,1)S(1)} %attend.3.refs_2_), channel_id=1, source_target_pairs={{0,2},{1,3},{2,0},{3,1},{4,6},{5,7},{6,4},{7,5},{8,10},{9,11},{10,... | collective-permute-start | bytes 491528 | tf_op jit(solution)/shard_map/ppermute | solution.py:390
  99.4 9.9 %collective-permute-start.31 = (bf16[256,320]{1,0:T(8,128)(2,1)S(1)}, bf16[256,320]{1,0:T(8,128)(2,1)S(1)}, u32[]{:S(2)}, u32[]{:S(2)}) collective-permute-start(bf16[256,320]{1,0:T(8,128)(2,1)S(1)} %attend.3.refs_2_), channel_id=1, source_target_pairs={{0,3},{1,2},{2,1},{3,0},{4,7},{5,6},{6,5},{7,4},{8,11},{9,10},{10,... | collective-permute-start | bytes 491528 | tf_op jit(solution)/shard_map/ppermute | solution.py:390
  105.0 13.2 %collective-permute-start.23 = (bf16[256,320]{1,0:T(8,128)(2,1)S(1)}, bf16[256,320]{1,0:T(8,128)(2,1)}, u32[]{:S(2)}, u32[]{:S(2)}) collective-permute-start(bf16[256,320]{1,0:T(8,128)(2,1)S(1)} %attend.2.refs_2_), channel_id=1, source_target_pairs={{0,1},{1,0},{2,3},{3,2},{4,5},{5,4},{6,7},{7,6},{8,9},{9,8},{10,11... | collective-permute-start | bytes 491528 | tf_op jit(solution)/shard_map/ppermute | solution.py:390
  105.8 12.4 %collective-permute-start.24 = (bf16[256,320]{1,0:T(8,128)(2,1)S(1)}, bf16[256,320]{1,0:T(8,128)(2,1)}, u32[]{:S(2)}, u32[]{:S(2)}) collective-permute-start(bf16[256,320]{1,0:T(8,128)(2,1)S(1)} %attend.2.refs_2_), channel_id=1, source_target_pairs={{0,2},{1,3},{2,0},{3,1},{4,6},{5,7},{6,4},{7,5},{8,10},{9,11},{10,... | collective-permute-start | bytes 491528 | tf_op jit(solution)/shard_map/ppermute | solution.py:390
  110.1 9.1 %collective-permute-start.25 = (bf16[256,320]{1,0:T(8,128)(2,1)S(1)}, bf16[256,320]{1,0:T(8,128)(2,1)}, u32[]{:S(2)}, u32[]{:S(2)}) collective-permute-start(bf16[256,320]{1,0:T(8,128)(2,1)S(1)} %attend.2.refs_2_), channel_id=1, source_target_pairs={{0,3},{1,2},{2,1},{3,0},{4,7},{5,6},{6,5},{7,4},{8,11},{9,10},{10,... | collective-permute-start | bytes 491528 | tf_op jit(solution)/shard_map/ppermute | solution.py:390
  (18 other events, 96.2 us)
where the time goes:
time: 126 us; the launch traced here: 124 us
  starting transfers between devices  54.2 us (43%)
  Pallas kernels  31.2 us (25%)
  waiting for transfers between devices  25 us (20%)
  local copies, waits for them, and re-layouts  10.7 us (8%)
  between operations  2.27 us (2%)
    ppermute x16, starting transfers between devices, fetch(): return lax.ppermute(array, 'req', pairs)  30.1 us
    ppermute x9, starting transfers between devices, across(): return lax.ppermute(array, 'tp', [(i, i ^ bit) for i in range(4)])  24.1 us
    ppermute x16, waiting for transfers between devices, fetch(): return lax.ppermute(array, 'req', pairs)  16.5 us
    unnamed x50, local copies, waits for them, and re-layouts  10.7 us
    pallas_call x2, Pallas kernels, local(): pl.pallas_call(lambda *refs, c=c: output_kernel(*refs, tile=256, start=c...  8.64 us
    pallas_call x2, Pallas kernels, local(): pl.pallas_call(lambda *refs: attend_kernel(*refs, tile=256), grid=(1,), o...  8.63 us
    ppermute x9, waiting for transfers between devices, across(): return lax.ppermute(array, 'tp', [(i, i ^ bit) for i in range(4)])  8.46 us
    pallas_call x1, Pallas kernels, local(): pl.pallas_call(lambda *refs: suffix_kernel(*refs, tile=256), out_shape=(s...  4.49 us
  transfers between devices with their start and end apart: 25, of which 11 were waited for; matrix products, arithmetic and copies ran while one was open for 0% of the time, Pallas kernels for 18%

commit v1 on v0

--- a/solution.py
+++ b/solution.py
@@ -48,6 +48,7 @@
     ),
 )
 CAP = 8
+SMALL = 64
 CHUNKS = 2
 
 
@@ -126,7 +127,7 @@
             kv_ref[h, rows] = jnp.where(first, keys, kv).astype(BF16)
 
 
-def suffix_kernel(len_ref, flag_ref, q_ref, kv_ref, acc_ref, peak_ref, *, tile):
+def suffix_kernel(len_ref, flag_ref, q_ref, kv_ref, acc_ref, *, tile):
     heads, suf, lanes = q_ref.shape
     first = lane_half(lanes)
     length = len_ref[0]
@@ -156,26 +157,24 @@
     @pl.when(jnp.logical_not(safe))
     def _():
         lane = lax.broadcasted_iota(jnp.int32, (1, lanes), 1)
-        peak_ref[...] = jnp.zeros_like(peak_ref)
-
-        def head(h, carry):
-            for i in range(suf // tile):
-                rows = slice(i * tile, (i + 1) * tile)
-                count = (i + 1) * tile
-                qpos = lax.broadcasted_iota(jnp.int32, (tile, count), 0) + i * tile
-                kpos = lax.broadcasted_iota(jnp.int32, (tile, count), 1)
-                keys = kv_ref[h, :count]
-                scores = jnp.where(
-                    (kpos <= qpos) & (kpos < length), dot_t(q_ref[h, rows], keys), -1e30
-                )
-                peak = jnp.max(scores, axis=-1, keepdims=True)
-                weights = jnp.exp2(scores - peak).astype(BF16)
-                ones_values = jnp.where(first, jnp.ones_like(keys), keys)
-                acc_ref[h, rows] = jnp.dot(weights, ones_values, preferred_element_type=F32)
-                peak_ref[rows] = jnp.where(lane == h, peak, peak_ref[rows])
+        pieces = suf // SMALL
+
+        def piece(n, carry):
+            h = n // pieces
+            row = pl.multiple_of((n % pieces) * SMALL, SMALL)
+            rows = pl.ds(row, SMALL)
+            qpos = lax.broadcasted_iota(jnp.int32, (SMALL, suf), 0) + row
+            kpos = lax.broadcasted_iota(jnp.int32, (SMALL, suf), 1)
+            keys = kv_ref[h]
+            scores = jnp.where((kpos <= qpos) & (kpos < length), dot_t(q_ref[h, rows], keys), -1e30)
+            peak = jnp.max(scores, axis=-1, keepdims=True)
+            weights = jnp.exp2(scores - peak).astype(BF16)
+            ones_values = jnp.where(first, jnp.ones_like(keys), keys)
+            total = jnp.dot(weights, ones_values, preferred_element_type=F32)
+            acc_ref[h, rows] = jnp.where(lane == 0, peak, total)
             return carry
 
-        lax.fori_loop(0, heads, head, 0)
+        lax.fori_loop(0, heads * pieces, piece, 0)
 
 
 def split_kernel(a_ref, b_ref, c_ref, d_ref, one_ref, two_ref):
@@ -305,8 +304,8 @@
     lax.fori_loop(0, 2 * slots, finish, 0)
 
 
-def attend_kernel(flag_ref, q_ref, acc_ref, peak_ref, kv_ref, out_ref, total_ref, *, tile):
-    heads, _, lanes = q_ref.shape
+def attend_kernel(flag_ref, q_ref, acc_ref, kv_ref, out_ref, total_ref, *, tile):
+    heads, rows, lanes = q_ref.shape
     size = lanes // 2
     count = kv_ref.shape[1]
     first = lane_half(lanes)
@@ -325,20 +324,24 @@
 
     @pl.when(jnp.logical_not(safe))
     def _():
-        lane = lax.broadcasted_iota(jnp.int32, (1, lanes), 1)
-
-        def head(h, carry):
+        pieces = rows // SMALL
+
+        def piece(n, carry):
+            h = n // pieces
+            part = pl.ds(pl.multiple_of((n % pieces) * SMALL, SMALL), SMALL)
             keys = kv_ref[h]
-            scores = dot_t(q_ref[h], keys)
-            near = jnp.max(jnp.where(lane == h, peak_ref[...], -3e38), axis=-1, keepdims=True)
+            held = acc_ref[h, part]
+            near = held[:, :1]
+            held = jnp.where(first, held[:, 1:2], held)
+            scores = dot_t(q_ref[h, part], keys)
             peak = jnp.maximum(jnp.max(scores, axis=-1, keepdims=True), near)
             weights = jnp.exp2(scores - peak).astype(BF16)
             ones_values = jnp.where(first, jnp.ones_like(keys), keys)
             total = jnp.dot(weights, ones_values, preferred_element_type=F32)
-            total_ref[h] = total + acc_ref[h] * jnp.exp2(near - peak)
+            total_ref[h, part] = total + held * jnp.exp2(near - peak)
             return carry
 
-        lax.fori_loop(0, heads, head, 0)
+        lax.fori_loop(0, heads * pieces, piece, 0)
 
     for h in range(heads):
         total = total_ref[h]
@@ -511,11 +514,11 @@
         compiler_params=vmem(14),
         cost_estimate=cost(2 * suf * width * 3 * heads * size, 0, 10_000_000),
     )(rows, w_query.T, w_key.T, w_value.T, key_scale)
-    acc, peaks = pl.pallas_call(
+    acc = pl.pallas_call(
         lambda *refs: suffix_kernel(*refs, tile=256),
-        out_shape=(shaped((heads, suf, lanes), F32), shaped((suf, lanes), F32)),
+        out_shape=shaped((heads, suf, lanes), F32),
         in_specs=[SMEM, SMEM, VMEM, VMEM],
-        out_specs=(VMEM, VMEM),
+        out_specs=VMEM,
         name="suffix",
         compiler_params=vmem(10),
         cost_estimate=cost(4 * suf * suf * heads * lanes, suf * suf * heads, 10_000_000),
@@ -537,7 +540,6 @@
                     SMEM,
                     pl.BlockSpec((heads, chunk, lanes), lambda i, c=c: (0, c, 0)),
                     pl.BlockSpec((heads, chunk, lanes), lambda i, c=c: (0, c, 0)),
-                    pl.BlockSpec((chunk, lanes), lambda i, c=c: (c, 0)),
                     VMEM,
                 ],
                 out_specs=pl.BlockSpec((chunk, heads * size), lambda i: (0, 0)),
@@ -545,7 +547,7 @@
                 name="attend",
         compiler_params=vmem(14),
                 cost_estimate=cost(4 * chunk * prefix_rows * heads * lanes, chunk * prefix_rows * heads, 8_000_000),
-            )(flag, q, acc, peaks, prefix)
+            )(flag, q, acc, prefix)
         )
     out = None
     for c in range(CHUNKS):

time: 126 us -> 153 us (1.21)
  Pallas kernels: 31.2 us -> 58.7 us
    pallas_call x2, Pallas kernels: 8.63 us -> 24 us  [local(): pl.pallas_call(lambda *refs: attend_kernel(*refs, tile=256), grid=(1,), o...]
    pallas_call x1, Pallas kernels: 4.49 us -> 16.6 us  [local(): pl.pallas_call(lambda *refs: suffix_kernel(*refs, tile=256), out_shape=sh...]
  transfers between devices with their start and end apart: 25 -> 25, of which waited for: 11 -> 10; matrix products, arithmetic and copies ran while one was open for 0% -> 0% of each run, Pallas kernels for 18% -> 33%
where the time goes in v1:
time: 153 us; the launch traced here: 150 us
  Pallas kernels  58.7 us (38%)
  starting transfers between devices  53.3 us (35%)
  waiting for transfers between devices  25 us (16%)
  local copies, waits for them, and re-layouts  10.7 us (7%)
  between operations  2.25 us (1%)
    ppermute x16, starting transfers between devices, fetch(): return lax.ppermute(array, 'req', pairs)  30.1 us
    pallas_call x2, Pallas kernels, local(): pl.pallas_call(lambda *refs: attend_kernel(*refs, tile=256), grid=(1,), o...  24 us
    ppermute x9, starting transfers between devices, across(): return lax.ppermute(array, 'tp', [(i, i ^ bit) for i in range(4)])  23.2 us
    pallas_call x1, Pallas kernels, local(): pl.pallas_call(lambda *refs: suffix_kernel(*refs, tile=256), out_shape=sh...  16.6 us
    ppermute x16, waiting for transfers between devices, fetch(): return lax.ppermute(array, 'req', pairs)  16.5 us
    unnamed x50, local copies, waits for them, and re-layouts  10.7 us
    pallas_call x2, Pallas kernels, local(): pl.pallas_call(lambda *refs, c=c: output_kernel(*refs, tile=256, start=c...  8.64 us
    ppermute x9, waiting for transfers between devices, across(): return lax.ppermute(array, 'tp', [(i, i ^ bit) for i in range(4)])  8.48 us
  transfers between devices with their start and end apart: 25, of which 10 were waited for; matrix products, arithmetic and copies ran while one was open for 0% of the time, Pallas kernels for 33%

profile of v1, /device:TPU:1, one launch (start us, length us, event | category | flops | bytes accessed | tf_op | source)
XLA Modules:
  0.0 150.2 jit_solution(13353251552893384175)
XLA Ops:
  2.9 2.1 %collective-permute-start.7 = (bf16[6,64,128]{2,1,0:T(8,128)(2,1)S(1)}, bf16[6,64,128]{2,1,0:T(8,128)(2,1)S(1)}, u32[]{:S(2)}, u32[]{:S(2)}) collective-permute-start(bf16[6,64,128]{2,1,0:T(8,128)(2,1)S(1)} %get-tuple-element.129.a_ref), channel_id=1, source_target_pairs={{128,0},{132,4},{136,8},{140,12},{144,16},{148,20},{152,24},{156,2... | collective-permute-start | bytes 294920 | tf_op jit(solution)/shard_map/ppermute | solution.py:34
  5.0 6.9 %collective-permute-start.8 = (bf16[6,64,128]{2,1,0:T(8,128)(2,1)S(1)}, bf16[6,64,128]{2,1,0:T(8,128)(2,1)S(1)}, u32[]{:S(2)}, u32[]{:S(2)}) collective-permute-start(bf16[6,64,128]{2,1,0:T(8,128)(2,1)S(1)} %get-tuple-element.129.a_ref), channel_id=1, source_target_pairs={{64,0},{68,4},{72,8},{76,12},{80,16},{84,20},{88,24},{92,28},{96,3... | collective-permute-start | bytes 294920 | tf_op jit(solution)/shard_map/ppermute | solution.py:34
  11.9 2.1 %collective-permute-done.8.c_ref = bf16[6,64,128]{2,1,0:T(8,128)(2,1)S(1)} collective-permute-done((bf16[6,64,128]{2,1,0:T(8,128)(2,1)S(1)}, bf16[6,64,128]{2,1,0:T(8,128)(2,1)S(1)}, u32[]{:S(2)}, u32[]{:S(2)}) %collective-permute-start.8) | collective-permute-done | bytes 98336 | tf_op jit(solution)/shard_map/ppermute | solution.py:34
  14.0 6.5 %collective-permute-done.9.d_ref = bf16[6,64,128]{2,1,0:T(8,128)(2,1)S(1)} collective-permute-done((bf16[6,64,128]{2,1,0:T(8,128)(2,1)S(1)}, bf16[6,64,128]{2,1,0:T(8,128)(2,1)S(1)}, u32[]{:S(2)}, u32[]{:S(2)}) %collective-permute-start.9) | collective-permute-done | bytes 98336 | tf_op jit(solution)/shard_map/ppermute | solution.py:34
  20.5 1.3 collective-permute-start.10
  23.6 3.5 %collective-permute-start.13 = (bf16[4,6,32,128]{3,2,1,0:T(8,128)(2,1)S(1)}, bf16[4,6,32,128]{3,2,1,0:T(8,128)(2,1)S(1)}, u32[]{:S(2)}, u32[]{:S(2)}) collective-permute-start(bf16[4,6,32,128]{3,2,1,0:T(8,128)(2,1)S(1)} %get-tuple-element.131.refs_6_), channel_id=1, source_target_pairs={{4,0},{8,4},{12,8},{0,12},{20,16},{24,20},{28,24},{16,28},{36,32},... | collective-permute-start | bytes 589832 | tf_op jit(solution)/shard_map/ppermute | solution.py:34
  27.1 2.9 %collective-permute-start.15 = (bf16[4,6,32,128]{3,2,1,0:T(8,128)(2,1)S(1)}, bf16[4,6,32,128]{3,2,1,0:T(8,128)(2,1)S(1)}, u32[]{:S(2)}, u32[]{:S(2)}) collective-permute-start(bf16[4,6,32,128]{3,2,1,0:T(8,128)(2,1)S(1)} %get-tuple-element.131.refs_6_), channel_id=1, source_target_pairs={{8,0},{12,4},{0,8},{4,12},{24,16},{28,20},{16,24},{20,28},{40,32},... | collective-permute-start | bytes 589832 | tf_op jit(solution)/shard_map/ppermute | solution.py:34
  31.3 2.8 %plan.1 = (s32[128]{0:T(128)S(1)}, s32[32]{0:T(128)S(1)}, s32[1]{0:T(128)}) custom-call(s32[1]{0:T(128)S(6)} %copy.17.member_ref.refs_0_, s32[1]{0:T(128)} %bitcast.6.place_ref, s32[4,16]{1,0:T(4,128)S(1)} %copy-done.9, s32[128]{0:T(128)S(1)} %copy-done.10), custom_call_target="tpu_custom_call" | custom-call | bytes 1000000 | tf_op jit(solution)/shard_map/plan/pallas_call | solution.py:413
  35.7 1.6 %pack.3 = (bf16[16,5,32,128]{3,2,1,0:T(8,128)(2,1)S(1)}, bf16[8,5,32,128]{3,2,1,0:T(8,128)(2,1)S(1)}, bf16[8,5,32,128]{3,2,1,0:T(8,128)(2,1)S(1)}, bf16[8,5,32,1...) custom-call(s32[1]{0:T(128)S(6)} %copy.17.member_ref.refs_0_, ...), custom_call_target="tpu_custom_call" | custom-call | bytes 4000000 | tf_op jit(solution)/shard_map/pack/pallas_call | solution.py:445
  37.3 2.8 %collective-permute-start.21 = (bf16[4,5,32,128]{3,2,1,0:T(8,128)(2,1)S(1)}, bf16[4,5,32,128]{3,2,1,0:T(8,128)(2,1)S(1)}, u32[]{:S(2)}, u32[]{:S(2)}) collective-permute-start(bf16[4,5,32,128]{3,2,1,0:T(8,128)(2,1)S(1)} %get-tuple-element.139), channel_id=1, source_target_pairs={{32,0},{36,4},{40,8},{44,12},{48,16},{52,20},{56,24},{60,28},{64,3... | collective-permute-start | bytes 491528 | tf_op jit(solution)/shard_map/ppermute | solution.py:34
  40.1 1.8 %collective-permute-start.16 = (bf16[8,5,32,128]{3,2,1,0:T(8,128)(2,1)S(1)}, bf16[8,5,32,128]{3,2,1,0:T(8,128)(2,1)S(1)}, u32[]{:S(2)}, u32[]{:S(2)}) collective-permute-start(bf16[8,5,32,128]{3,2,1,0:T(8,128)(2,1)S(1)} %get-tuple-element.133), channel_id=1, source_target_pairs={{4,0},{8,4},{12,8},{0,12},{20,16},{24,20},{28,24},{16,28},{36,32},... | collective-permute-start | bytes 983048 | tf_op jit(solution)/shard_map/ppermute | solution.py:34
  41.9 2.0 %collective-permute-start.18 = (bf16[8,5,32,128]{3,2,1,0:T(8,128)(2,1)S(1)}, bf16[8,5,32,128]{3,2,1,0:T(8,128)(2,1)S(1)}, u32[]{:S(2)}, u32[]{:S(2)}) collective-permute-start(bf16[8,5,32,128]{3,2,1,0:T(8,128)(2,1)S(1)} %get-tuple-element.135), channel_id=1, source_target_pairs={{8,0},{12,4},{0,8},{4,12},{24,16},{28,20},{16,24},{20,28},{40,32},... | collective-permute-start | bytes 983048 | tf_op jit(solution)/shard_map/ppermute | solution.py:34
  44.3 3.3 %collective-permute-start.19 = (bf16[8,5,32,128]{3,2,1,0:T(8,128)(2,1)S(1)}, bf16[8,5,32,128]{3,2,1,0:T(8,128)(2,1)S(1)}, u32[]{:S(2)}, u32[]{:S(2)}) collective-permute-start(bf16[8,5,32,128]{3,2,1,0:T(8,128)(2,1)S(1)} %get-tuple-element.137), channel_id=1, source_target_pairs={{16,0},{20,4},{24,8},{28,12},{32,16},{36,20},{40,24},{44,28},{48,3... | collective-permute-start | bytes 983048 | tf_op jit(solution)/shard_map/ppermute | solution.py:34
  47.6 1.8 %collective-permute-start.20 = (bf16[8,5,32,128]{3,2,1,0:T(8,128)(2,1)S(1)}, bf16[8,5,32,128]{3,2,1,0:T(8,128)(2,1)S(1)}, u32[]{:S(2)}, u32[]{:S(2)}) collective-permute-start(bf16[8,5,32,128]{3,2,1,0:T(8,128)(2,1)S(1)} %get-tuple-element.138), channel_id=1, source_target_pairs={{112,0},{116,4},{120,8},{124,12},{0,16},{4,20},{8,24},{12,28},{16,... | collective-permute-start | bytes 983048 | tf_op jit(solution)/shard_map/ppermute | solution.py:34
  50.0 1.2 collective-permute-done.17
  51.2 3.1 %collective-permute-done.18 = bf16[8,5,32,128]{3,2,1,0:T(8,128)(2,1)S(1)} collective-permute-done((bf16[8,5,32,128]{3,2,1,0:T(8,128)(2,1)S(1)}, bf16[8,5,32,128]{3,2,1,0:T(8,128)(2,1)S(1)}, u32[]{:S(2)}, u32[]{:S(2)}) %collective-permute-start.18) | collective-permute-done | bytes 327712 | tf_op jit(solution)/shard_map/ppermute | solution.py:34
  54.4 1.6 %collective-permute-done.20 = bf16[8,5,32,128]{3,2,1,0:T(8,128)(2,1)S(1)} collective-permute-done((bf16[8,5,32,128]{3,2,1,0:T(8,128)(2,1)S(1)}, bf16[8,5,32,128]{3,2,1,0:T(8,128)(2,1)S(1)}, u32[]{:S(2)}, u32[]{:S(2)}) %collective-permute-start.20) | collective-permute-done | bytes 327712 | tf_op jit(solution)/shard_map/ppermute | solution.py:34
  56.1 2.6 %conditional.1 = (bf16[5,1024,128]{2,1,0:T(8,128)(2,1)S(1)}) conditional(s32[]{:T(128)} %bitcast.7, (s32[32]{0:T(128)S(1)}, bf16[16,5,32,128]{3,2,1,0:T(8,128)(2,1)S(1)}, bf16[8,5,32,128]{3,2,1,0:T(8,128)(2,1)S(1)}, bf16[8,5,32,128]{3,2,1,0:T(8,128)(2,1)S(1)}, bf16[8,5,32,128]{3,2,1,0:T(8,128)(2,1)S(1)}, ...), branch_computations={%region_0.0_spmd, %region_1.0_spmd} | conditional | bytes 14864608 | solution.py:470
  56.1 2.4 %select.2 = bf16[5,1024,128]{2,1,0:T(8,128)(2,1)S(1)} custom-call(s32[32]{0:T(128)S(1)} %get-tuple-element.68.recv_ref, bf16[16,5,32,128]{3,2,1,0:T(8,128)(2,1)S(1)} %get-tuple-element.69.rest_0_, bf16[8,5,32,128]{3,2,1,0:T(8,128)(2,1)S(1)} %get-tuple-element.70.rest_1_, bf16[8,5,32,128]{3,2,1,0:T(8,128)(2,1)S(1)} %get-tuple-element.71.rest_2_, ...), custom_call_target="tpu_custom_call" | custom-call | bytes 3000000 | tf_op jit(solution)/shard_map/cond/branch_0_fun/select/pallas_call | solution.py:458
  59.8 2.4 %collective-permute-start.27 = (bf16[320,1280]{1,0:T(8,128)(2,1)S(1)}, bf16[320,1280]{1,0:T(8,128)(2,1)S(1)}, u32[]{:S(2)}, u32[]{:S(2)}) collective-permute-start(bf16[320,1280]{1,0:T(8,128)(2,1)S(1)} %copy-done.1), channel_id=1, source_target_pairs={{0,2},{1,3},{2,0},{3,1},{4,6},{5,7},{6,4},{7,5},{8,10},{9,11},{10,... | collective-permute-start | bytes 2457608 | tf_op jit(solution)/shard_map/ppermute | solution.py:393
  62.2 6.5 %collective-permute-start.26 = (bf16[320,1280]{1,0:T(8,128)(2,1)S(1)}, bf16[320,1280]{1,0:T(8,128)(2,1)}, u32[]{:S(2)}, u32[]{:S(2)}) collective-permute-start(bf16[320,1280]{1,0:T(8,128)(2,1)S(1)} %copy-done.1), channel_id=1, source_target_pairs={{0,1},{1,0},{2,3},{3,2},{4,5},{5,4},{6,7},{7,6},{8,9},{9,8},{10,11... | collective-permute-start | bytes 2457608 | tf_op jit(solution)/shard_map/ppermute | solution.py:393
  68.7 6.4 %collective-permute-done.27.refs_8_ = bf16[320,1280]{1,0:T(8,128)(2,1)S(1)} collective-permute-done((bf16[320,1280]{1,0:T(8,128)(2,1)S(1)}, bf16[320,1280]{1,0:T(8,128)(2,1)S(1)}, u32[]{:S(2)}, u32[]{:S(2)}) %collective-permute-start.27) | collective-permute-done | bytes 819232 | tf_op jit(solution)/shard_map/ppermute | solution.py:393
  75.1 6.9 %collective-permute-start.28 = (bf16[320,1280]{1,0:T(8,128)(2,1)S(1)}, bf16[320,1280]{1,0:T(8,128)(2,1)}, u32[]{:S(2)}, u32[]{:S(2)}) collective-permute-start(bf16[320,1280]{1,0:T(8,128)(2,1)S(1)} %collective-permute-done.27.refs_8_), channel_id=1, source_target_pairs={{0,1},{1,0},{2,3},{3,2},{4,5},{5,4},{6,7},{7,6},{8,9},{9,8},{10,11... | collective-permute-start | bytes 2457608 | tf_op jit(solution)/shard_map/ppermute | solution.py:393
  86.1 2.0 %qkv.1 = (bf16[5,512,128]{2,1,0:T(8,128)(2,1)S(1)}, bf16[5,512,128]{2,1,0:T(8,128)(2,1)S(1)}) custom-call(bf16[512,1280]{1,0:T(8,128)(2,1)S(1)} %bitcast.11, bf16[320,1280]{1,0:T(8,128)(2,1)S(1)} %bitcast.15, bf16[320,1280]{1,0:T(8,128)(2,1)S(1)} %bitcast.16, bf16[320,1280]{1,0:T(8,128)(2,1)S(1)} %bitcast.17, f32[5,64]{1,0:T(8,128)S(1)} %copy-done.8), custom_call_target="tpu_custom_call" | custom-call | flops 1258291200 | bytes 10000000 | tf_op jit(solution)/shard_map/qkv/pallas_call | solution.py:507
  88.1 16.6 %suffix.1.refs_2_ = f32[5,512,128]{2,1,0:T(8,128)S(1)} custom-call(s32[1]{0:T(128)S(6)} %copy.18.refs_0_, s32[1]{0:T(128)} %get-tuple-element.123.refs_1_.refs_0_, bf16[5,512,128]{2,1,0:T(8,128)(2,1)S(1)} %get-tuple-element.124.refs_2_.refs_1_, bf16[5,512,128]{2,1,0:T(8,128)(2,1)S(1)} %get-tuple-element.125.refs_3_), custom_call_target="tpu_custom_call" | custom-call | flops 671088640 | bytes 10000000 | tf_op jit(solution)/shard_map/suffix/pallas_call | solution.py:517
  104.8 12.0 %attend.3.refs_2_ = bf16[256,320]{1,0:T(8,128)(2,1)S(1)} custom-call(s32[1]{0:T(128)} %get-tuple-element.123.refs_1_.refs_0_, bf16[5,512,128]{2,1,0:T(8,128)(2,1)S(1)} %get-tuple-element.124.refs_2_.refs_1_, f32[5,512,128]{2,1,0:T(8,128)S(1)} %suffix.1.refs_2_, bf16[5,1024,128]{2,1,0:T(8,128)(2,1)S(1)} %copy-done.15), custom_call_target="tpu_custom_call" | custom-call | flops 671088640 | bytes 8000000 | tf_op jit(solution)/shard_map/attend/pallas_call | solution.py:535
  116.9 2.5 %collective-permute-start.30 = (bf16[256,320]{1,0:T(8,128)(2,1)S(1)}, bf16[256,320]{1,0:T(8,128)(2,1)S(1)}, u32[]{:S(2)}, u32[]{:S(2)}) collective-permute-start(bf16[256,320]{1,0:T(8,128)(2,1)S(1)} %attend.3.refs_2_), channel_id=1, source_target_pairs={{0,2},{1,3},{2,0},{3,1},{4,6},{5,7},{6,4},{7,5},{8,10},{9,11},{10,... | collective-permute-start | bytes 491528 | tf_op jit(solution)/shard_map/ppermute | solution.py:393
  120.5 12.0 %attend.2.refs_2_ = bf16[256,320]{1,0:T(8,128)(2,1)S(1)} custom-call(s32[1]{0:T(128)} %get-tuple-element.123.refs_1_.refs_0_, bf16[5,512,128]{2,1,0:T(8,128)(2,1)S(1)} %get-tuple-element.124.refs_2_.refs_1_, f32[5,512,128]{2,1,0:T(8,128)S(1)} %suffix.1.refs_2_, bf16[5,1024,128]{2,1,0:T(8,128)(2,1)S(1)} %copy-done.15), custom_call_target="tpu_custom_call" | custom-call | flops 671088640 | bytes 8000000 | tf_op jit(solution)/shard_map/attend/pallas_call | solution.py:535
  133.4 2.4 %collective-permute-start.24 = (bf16[256,320]{1,0:T(8,128)(2,1)S(1)}, bf16[256,320]{1,0:T(8,128)(2,1)}, u32[]{:S(2)}, u32[]{:S(2)}) collective-permute-start(bf16[256,320]{1,0:T(8,128)(2,1)S(1)} %attend.2.refs_2_), channel_id=1, source_target_pairs={{0,2},{1,3},{2,0},{3,1},{4,6},{5,7},{6,4},{7,5},{8,10},{9,11},{10,... | collective-permute-start | bytes 491528 | tf_op jit(solution)/shard_map/ppermute | solution.py:393
  139.5 4.2 %output.2.refs_12_ = bf16[320,512]{1,0:T(8,128)(2,1)} custom-call(s32[1]{0:T(128)S(6)} %copy.18.refs_0_, s32[1]{0:T(128)} %bitcast.refs_1_, bf16[256,320]{1,0:T(8,128)(2,1)S(1)} %attend.3.refs_2_, bf16[256,320]{1,0:T(8,128)(2,1)S(1)} %collective-permute-done.29.refs_3_, bf16[256,320]{1,0:T(8,128)(2,1)S(1)} %copy-done.3, bf16[256,320]{1,0:T(8,128)(2,1)S(1)} %copy-done.5, ...), custom_call_target="tpu_custom_call" | custom-call | flops 838860800 | bytes 6000000 | tf_op jit(solution)/shard_map/output/pallas_call | solution.py:564
  143.8 2.0 %collective-permute-done.25.refs_5_ = bf16[256,320]{1,0:T(8,128)(2,1)} collective-permute-done((bf16[256,320]{1,0:T(8,128)(2,1)S(1)}, bf16[256,320]{1,0:T(8,128)(2,1)}, u32[]{:S(2)}, u32[]{:S(2)}) %collective-permute-start.25) | collective-permute-done | bytes 163872 | tf_op jit(solution)/shard_map/ppermute | solution.py:393
  145.8 4.4 %output.3 = bf16[320,512]{1,0:T(8,128)(2,1)} custom-call(s32[1]{0:T(128)S(6)} %copy.18.refs_0_, s32[1]{0:T(128)} %bitcast.refs_1_, bf16[256,320]{1,0:T(8,128)(2,1)S(1)} %attend.2.refs_2_, bf16[256,320]{1,0:T(8,128)(2,1)} %collective-permute-done.23.refs_3_, bf16[256,320]{1,0:T(8,128)(2,1)} %collective-permute-done.24.refs_4_, ...), custom_call_target="tpu_custom_call", output_to_operand_aliasing={{}: (12, {})} | custom-call | flops 838860800 | bytes 6000000 | tf_op jit(solution)/shard_map/output/pallas_call | solution.py:564
  (81 shorter events, 17.7 us)
Async XLA Ops:
  2.9 9.0 %collective-permute-start.7 = (bf16[6,64,128]{2,1,0:T(8,128)(2,1)S(1)}, bf16[6,64,128]{2,1,0:T(8,128)(2,1)S(1)}, u32[]{:S(2)}, u32[]{:S(2)}) collective-permute-start(bf16[6,64,128]{2,1,0:T(8,128)(2,1)S(1)} %get-tuple-element.129.a_ref), channel_id=1, source_target_pairs={{128,0},{132,4},{136,8},{140,12},{144,16},{148,20},{152,24},{156,2... | collective-permute-start | bytes 294920 | tf_op jit(solution)/shard_map/ppermute | solution.py:34
  5.0 9.0 %collective-permute-start.8 = (bf16[6,64,128]{2,1,0:T(8,128)(2,1)S(1)}, bf16[6,64,128]{2,1,0:T(8,128)(2,1)S(1)}, u32[]{:S(2)}, u32[]{:S(2)}) collective-permute-start(bf16[6,64,128]{2,1,0:T(8,128)(2,1)S(1)} %get-tuple-element.129.a_ref), channel_id=1, source_target_pairs={{64,0},{68,4},{72,8},{76,12},{80,16},{84,20},{88,24},{92,28},{96,3... | collective-permute-start | bytes 294920 | tf_op jit(solution)/shard_map/ppermute | solution.py:34
  11.9 8.6 %collective-permute-start.9 = (bf16[6,64,128]{2,1,0:T(8,128)(2,1)S(1)}, bf16[6,64,128]{2,1,0:T(8,128)(2,1)S(1)}, u32[]{:S(2)}, u32[]{:S(2)}) collective-permute-start(bf16[6,64,128]{2,1,0:T(8,128)(2,1)S(1)} %get-tuple-element.129.a_ref), channel_id=1, source_target_pairs={{192,0},{196,4},{200,8},{204,12},{208,16},{212,20},{216,24},{220,2... | collective-permute-start | bytes 294920 | tf_op jit(solution)/shard_map/ppermute | solution.py:34
  20.5 35.5 %copy-start.16 = (bf16[4,6,32,128]{3,2,1,0:T(8,128)(2,1)}, bf16[4,6,32,128]{3,2,1,0:T(8,128)(2,1)S(1)}, u32[]{:S(2)}) copy-start(bf16[4,6,32,128]{3,2,1,0:T(8,128)(2,1)S(1)} %get-tuple-element.130.refs_2_) | copy-start | bytes 589828
  20.5 35.5 %copy-start.17 = (bf16[4,6,32,128]{3,2,1,0:T(8,128)(2,1)}, bf16[4,6,32,128]{3,2,1,0:T(8,128)(2,1)S(1)}, u32[]{:S(2)}) copy-start(bf16[4,6,32,128]{3,2,1,0:T(8,128)(2,1)S(1)} %get-tuple-element.131.refs_6_) | copy-start | bytes 589828
  20.5 6.6 %collective-permute-start.10 = (bf16[4,6,32,128]{3,2,1,0:T(8,128)(2,1)S(1)}, bf16[4,6,32,128]{3,2,1,0:T(8,128)(2,1)S(1)}, u32[]{:S(2)}, u32[]{:S(2)}) collective-permute-start(bf16[4,6,32,128]{3,2,1,0:T(8,128)(2,1)S(1)} %get-tuple-element.130.refs_2_), channel_id=1, source_target_pairs={{16,0},{20,4},{24,8},{28,12},{32,16},{36,20},{40,24},{44,28},{48,3... | collective-permute-start | bytes 589832 | tf_op jit(solution)/shard_map/ppermute | solution.py:34
  21.8 12.3 %collective-permute-start.11 = (bf16[4,6,32,128]{3,2,1,0:T(8,128)(2,1)S(1)}, bf16[4,6,32,128]{3,2,1,0:T(8,128)(2,1)S(1)}, u32[]{:S(2)}, u32[]{:S(2)}) collective-permute-start(bf16[4,6,32,128]{3,2,1,0:T(8,128)(2,1)S(1)} %get-tuple-element.130.refs_2_), channel_id=1, source_target_pairs={{112,0},{116,4},{120,8},{124,12},{0,16},{4,20},{8,24},{12,28},{16,... | collective-permute-start | bytes 589832 | tf_op jit(solution)/shard_map/ppermute | solution.py:34
  22.5 12.2 %collective-permute-start.12 = (bf16[4,6,32,128]{3,2,1,0:T(8,128)(2,1)S(1)}, bf16[4,6,32,128]{3,2,1,0:T(8,128)(2,1)S(1)}, u32[]{:S(2)}, u32[]{:S(2)}) collective-permute-start(bf16[4,6,32,128]{3,2,1,0:T(8,128)(2,1)S(1)} %get-tuple-element.130.refs_2_), channel_id=1, source_target_pairs={{96,0},{100,4},{104,8},{108,12},{112,16},{116,20},{120,24},{124,28... | collective-permute-start | bytes 589832 | tf_op jit(solution)/shard_map/ppermute | solution.py:34
  23.6 11.1 %collective-permute-start.13 = (bf16[4,6,32,128]{3,2,1,0:T(8,128)(2,1)S(1)}, bf16[4,6,32,128]{3,2,1,0:T(8,128)(2,1)S(1)}, u32[]{:S(2)}, u32[]{:S(2)}) collective-permute-start(bf16[4,6,32,128]{3,2,1,0:T(8,128)(2,1)S(1)} %get-tuple-element.131.refs_6_), channel_id=1, source_target_pairs={{4,0},{8,4},{12,8},{0,12},{20,16},{24,20},{28,24},{16,28},{36,32},... | collective-permute-start | bytes 589832 | tf_op jit(solution)/shard_map/ppermute | solution.py:34
  27.1 8.6 %collective-permute-start.14 = (bf16[4,6,32,128]{3,2,1,0:T(8,128)(2,1)S(1)}, bf16[4,6,32,128]{3,2,1,0:T(8,128)(2,1)S(1)}, u32[]{:S(2)}, u32[]{:S(2)}) collective-permute-start(bf16[4,6,32,128]{3,2,1,0:T(8,128)(2,1)S(1)} %get-tuple-element.131.refs_6_), channel_id=1, source_target_pairs={{12,0},{0,4},{4,8},{8,12},{28,16},{16,20},{20,24},{24,28},{44,32},... | collective-permute-start | bytes 589832 | tf_op jit(solution)/shard_map/ppermute | solution.py:34
  27.1 28.9 %copy-start.18 = (bf16[4,6,32,128]{3,2,1,0:T(8,128)(2,1)}, bf16[4,6,32,128]{3,2,1,0:T(8,128)(2,1)S(1)}, u32[]{:S(2)}) copy-start(bf16[4,6,32,128]{3,2,1,0:T(8,128)(2,1)S(1)} %collective-permute-done.10.refs_3_) | copy-start | bytes 589828
  27.1 8.6 %collective-permute-start.15 = (bf16[4,6,32,128]{3,2,1,0:T(8,128)(2,1)S(1)}, bf16[4,6,32,128]{3,2,1,0:T(8,128)(2,1)S(1)}, u32[]{:S(2)}, u32[]{:S(2)}) collective-permute-start(bf16[4,6,32,128]{3,2,1,0:T(8,128)(2,1)S(1)} %get-tuple-element.131.refs_6_), channel_id=1, source_target_pairs={{8,0},{12,4},{0,8},{4,12},{24,16},{28,20},{16,24},{20,28},{40,32},... | collective-permute-start | bytes 589832 | tf_op jit(solution)/shard_map/ppermute | solution.py:34
  34.1 21.9 %copy-start.19 = (bf16[4,6,32,128]{3,2,1,0:T(8,128)(2,1)}, bf16[4,6,32,128]{3,2,1,0:T(8,128)(2,1)S(1)}, u32[]{:S(2)}) copy-start(bf16[4,6,32,128]{3,2,1,0:T(8,128)(2,1)S(1)} %collective-permute-done.11.refs_4_) | copy-start | bytes 589828
  34.7 21.3 %copy-start.21 = (bf16[4,6,32,128]{3,2,1,0:T(8,128)(2,1)}, bf16[4,6,32,128]{3,2,1,0:T(8,128)(2,1)S(1)}, u32[]{:S(2)}) copy-start(bf16[4,6,32,128]{3,2,1,0:T(8,128)(2,1)S(1)} %collective-permute-done.13.refs_7_) | copy-start | bytes 589828
  37.3 7.0 %collective-permute-start.21 = (bf16[4,5,32,128]{3,2,1,0:T(8,128)(2,1)S(1)}, bf16[4,5,32,128]{3,2,1,0:T(8,128)(2,1)S(1)}, u32[]{:S(2)}, u32[]{:S(2)}) collective-permute-start(bf16[4,5,32,128]{3,2,1,0:T(8,128)(2,1)S(1)} %get-tuple-element.139), channel_id=1, source_target_pairs={{32,0},{36,4},{40,8},{44,12},{48,16},{52,20},{56,24},{60,28},{64,3... | collective-permute-start | bytes 491528 | tf_op jit(solution)/shard_map/ppermute | solution.py:34
  40.1 7.5 %collective-permute-start.22 = (bf16[4,5,32,128]{3,2,1,0:T(8,128)(2,1)S(1)}, bf16[4,5,32,128]{3,2,1,0:T(8,128)(2,1)S(1)}, u32[]{:S(2)}, u32[]{:S(2)}) collective-permute-start(bf16[4,5,32,128]{3,2,1,0:T(8,128)(2,1)S(1)} %get-tuple-element.140), channel_id=1, source_target_pairs={{96,0},{100,4},{104,8},{108,12},{112,16},{116,20},{120,24},{124,28... | collective-permute-start | bytes 491528 | tf_op jit(solution)/shard_map/ppermute | solution.py:34
  40.1 9.9 %collective-permute-start.16 = (bf16[8,5,32,128]{3,2,1,0:T(8,128)(2,1)S(1)}, bf16[8,5,32,128]{3,2,1,0:T(8,128)(2,1)S(1)}, u32[]{:S(2)}, u32[]{:S(2)}) collective-permute-start(bf16[8,5,32,128]{3,2,1,0:T(8,128)(2,1)S(1)} %get-tuple-element.133), channel_id=1, source_target_pairs={{4,0},{8,4},{12,8},{0,12},{20,16},{24,20},{28,24},{16,28},{36,32},... | collective-permute-start | bytes 983048 | tf_op jit(solution)/shard_map/ppermute | solution.py:34
  41.9 9.4 %collective-permute-start.17 = (bf16[8,5,32,128]{3,2,1,0:T(8,128)(2,1)S(1)}, bf16[8,5,32,128]{3,2,1,0:T(8,128)(2,1)S(1)}, u32[]{:S(2)}, u32[]{:S(2)}) collective-permute-start(bf16[8,5,32,128]{3,2,1,0:T(8,128)(2,1)S(1)} %get-tuple-element.134), channel_id=1, source_target_pairs={{12,0},{0,4},{4,8},{8,12},{28,16},{16,20},{20,24},{24,28},{44,32},... | collective-permute-start | bytes 983048 | tf_op jit(solution)/shard_map/ppermute | solution.py:34
  41.9 12.5 %collective-permute-start.18 = (bf16[8,5,32,128]{3,2,1,0:T(8,128)(2,1)S(1)}, bf16[8,5,32,128]{3,2,1,0:T(8,128)(2,1)S(1)}, u32[]{:S(2)}, u32[]{:S(2)}) collective-permute-start(bf16[8,5,32,128]{3,2,1,0:T(8,128)(2,1)S(1)} %get-tuple-element.135), channel_id=1, source_target_pairs={{8,0},{12,4},{0,8},{4,12},{24,16},{28,20},{16,24},{20,28},{40,32},... | collective-permute-start | bytes 983048 | tf_op jit(solution)/shard_map/ppermute | solution.py:34
  44.3 10.1 %collective-permute-start.19 = (bf16[8,5,32,128]{3,2,1,0:T(8,128)(2,1)S(1)}, bf16[8,5,32,128]{3,2,1,0:T(8,128)(2,1)S(1)}, u32[]{:S(2)}, u32[]{:S(2)}) collective-permute-start(bf16[8,5,32,128]{3,2,1,0:T(8,128)(2,1)S(1)} %get-tuple-element.137), channel_id=1, source_target_pairs={{16,0},{20,4},{24,8},{28,12},{32,16},{36,20},{40,24},{44,28},{48,3... | collective-permute-start | bytes 983048 | tf_op jit(solution)/shard_map/ppermute | solution.py:34
  47.6 8.4 %collective-permute-start.20 = (bf16[8,5,32,128]{3,2,1,0:T(8,128)(2,1)S(1)}, bf16[8,5,32,128]{3,2,1,0:T(8,128)(2,1)S(1)}, u32[]{:S(2)}, u32[]{:S(2)}) collective-permute-start(bf16[8,5,32,128]{3,2,1,0:T(8,128)(2,1)S(1)} %get-tuple-element.138), channel_id=1, source_target_pairs={{112,0},{116,4},{120,8},{124,12},{0,16},{4,20},{8,24},{12,28},{16,... | collective-permute-start | bytes 983048 | tf_op jit(solution)/shard_map/ppermute | solution.py:34
  56.1 26.6 %copy-start = (bf16[1,512,1280]{2,1,0:T(8,128)(2,1)S(1)}, bf16[1,512,1280]{2,1,0:T(8,128)(2,1)}, u32[]{:S(2)}) copy-start(bf16[1,512,1280]{2,1,0:T(8,128)(2,1)} %param.14) | copy-start | bytes 3932164
  56.1 26.6 %copy-start.8 = (f32[5,64]{1,0:T(8,128)S(1)}, f32[5,64]{1,0:T(8,128)}, u32[]{:S(2)}) copy-start(f32[5,64]{1,0:T(8,128)} %refs_4_.1) | copy-start | bytes 3844
  59.8 15.3 %collective-permute-start.27 = (bf16[320,1280]{1,0:T(8,128)(2,1)S(1)}, bf16[320,1280]{1,0:T(8,128)(2,1)S(1)}, u32[]{:S(2)}, u32[]{:S(2)}) collective-permute-start(bf16[320,1280]{1,0:T(8,128)(2,1)S(1)} %copy-done.1), channel_id=1, source_target_pairs={{0,2},{1,3},{2,0},{3,1},{4,6},{5,7},{6,4},{7,5},{8,10},{9,11},{10,... | collective-permute-start | bytes 2457608 | tf_op jit(solution)/shard_map/ppermute | solution.py:393
  62.2 75.5 %collective-permute-start.26 = (bf16[320,1280]{1,0:T(8,128)(2,1)S(1)}, bf16[320,1280]{1,0:T(8,128)(2,1)}, u32[]{:S(2)}, u32[]{:S(2)}) collective-permute-start(bf16[320,1280]{1,0:T(8,128)(2,1)S(1)} %copy-done.1), channel_id=1, source_target_pairs={{0,1},{1,0},{2,3},{3,2},{4,5},{5,4},{6,7},{7,6},{8,9},{9,8},{10,11... | collective-permute-start | bytes 2457608 | tf_op jit(solution)/shard_map/ppermute | solution.py:393
  75.1 62.6 %collective-permute-start.28 = (bf16[320,1280]{1,0:T(8,128)(2,1)S(1)}, bf16[320,1280]{1,0:T(8,128)(2,1)}, u32[]{:S(2)}, u32[]{:S(2)}) collective-permute-start(bf16[320,1280]{1,0:T(8,128)(2,1)S(1)} %collective-permute-done.27.refs_8_), channel_id=1, source_target_pairs={{0,1},{1,0},{2,3},{3,2},{4,5},{5,4},{6,7},{7,6},{8,9},{9,8},{10,11... | collective-permute-start | bytes 2457608 | tf_op jit(solution)/shard_map/ppermute | solution.py:393
  116.8 15.8 %collective-permute-start.29 = (bf16[256,320]{1,0:T(8,128)(2,1)S(1)}, bf16[256,320]{1,0:T(8,128)(2,1)S(1)}, u32[]{:S(2)}, u32[]{:S(2)}) collective-permute-start(bf16[256,320]{1,0:T(8,128)(2,1)S(1)} %attend.3.refs_2_), channel_id=1, source_target_pairs={{0,1},{1,0},{2,3},{3,2},{4,5},{5,4},{6,7},{7,6},{8,9},{9,8},{10,11... | collective-permute-start | bytes 491528 | tf_op jit(solution)/shard_map/ppermute | solution.py:393
  116.9 15.8 %collective-permute-start.30 = (bf16[256,320]{1,0:T(8,128)(2,1)S(1)}, bf16[256,320]{1,0:T(8,128)(2,1)S(1)}, u32[]{:S(2)}, u32[]{:S(2)}) collective-permute-start(bf16[256,320]{1,0:T(8,128)(2,1)S(1)} %attend.3.refs_2_), channel_id=1, source_target_pairs={{0,2},{1,3},{2,0},{3,1},{4,6},{5,7},{6,4},{7,5},{8,10},{9,11},{10,... | collective-permute-start | bytes 491528 | tf_op jit(solution)/shard_map/ppermute | solution.py:393
  119.4 16.4 %collective-permute-start.31 = (bf16[256,320]{1,0:T(8,128)(2,1)S(1)}, bf16[256,320]{1,0:T(8,128)(2,1)S(1)}, u32[]{:S(2)}, u32[]{:S(2)}) collective-permute-start(bf16[256,320]{1,0:T(8,128)(2,1)S(1)} %attend.3.refs_2_), channel_id=1, source_target_pairs={{0,3},{1,2},{2,1},{3,0},{4,7},{5,6},{6,5},{7,4},{8,11},{9,10},{10,... | collective-permute-start | bytes 491528 | tf_op jit(solution)/shard_map/ppermute | solution.py:393
  132.6 11.2 %collective-permute-start.23 = (bf16[256,320]{1,0:T(8,128)(2,1)S(1)}, bf16[256,320]{1,0:T(8,128)(2,1)}, u32[]{:S(2)}, u32[]{:S(2)}) collective-permute-start(bf16[256,320]{1,0:T(8,128)(2,1)S(1)} %attend.2.refs_2_), channel_id=1, source_target_pairs={{0,1},{1,0},{2,3},{3,2},{4,5},{5,4},{6,7},{7,6},{8,9},{9,8},{10,11... | collective-permute-start | bytes 491528 | tf_op jit(solution)/shard_map/ppermute | solution.py:393
  133.4 10.4 %collective-permute-start.24 = (bf16[256,320]{1,0:T(8,128)(2,1)S(1)}, bf16[256,320]{1,0:T(8,128)(2,1)}, u32[]{:S(2)}, u32[]{:S(2)}) collective-permute-start(bf16[256,320]{1,0:T(8,128)(2,1)S(1)} %attend.2.refs_2_), channel_id=1, source_target_pairs={{0,2},{1,3},{2,0},{3,1},{4,6},{5,7},{6,4},{7,5},{8,10},{9,11},{10,... | collective-permute-start | bytes 491528 | tf_op jit(solution)/shard_map/ppermute | solution.py:393
  136.5 9.3 %collective-permute-start.25 = (bf16[256,320]{1,0:T(8,128)(2,1)S(1)}, bf16[256,320]{1,0:T(8,128)(2,1)}, u32[]{:S(2)}, u32[]{:S(2)}) collective-permute-start(bf16[256,320]{1,0:T(8,128)(2,1)S(1)} %attend.2.refs_2_), channel_id=1, source_target_pairs={{0,3},{1,2},{2,1},{3,0},{4,7},{5,6},{6,5},{7,4},{8,11},{9,10},{10,... | collective-permute-start | bytes 491528 | tf_op jit(solution)/shard_map/ppermute | solution.py:393
  (18 other events, 113.9 us)

commit v2 on v1

--- a/solution.py
+++ b/solution.py
@@ -499,7 +499,6 @@
         in_specs=[SMEM, VMEM, VMEM],
         out_specs=(SMEM, VMEM),
         name="prep",
-        compiler_params=vmem(2),
         cost_estimate=cost(0, 0, 300_000),
     )(membership, jnp.transpose(prefix_cache, (1, 0, 2)), key_scale)
     prefix = gather_prefix(whole, membership, owners)
@@ -533,7 +532,7 @@
     for c in range(CHUNKS):
         attended.append(
             pl.pallas_call(
-                lambda *refs: attend_kernel(*refs, tile=256),
+                lambda *refs: attend_kernel(*refs, tile=1024),
                 grid=(1,),
                 out_shape=shaped((chunk, heads * size), BF16),
                 in_specs=[
@@ -544,8 +543,7 @@
                 ],
                 out_specs=pl.BlockSpec((chunk, heads * size), lambda i: (0, 0)),
                 scratch_shapes=[pltpu.VMEM((heads, chunk, lanes), F32)],
-                name="attend",
-        compiler_params=vmem(14),
+                compiler_params=vmem(14),
                 cost_estimate=cost(4 * chunk * prefix_rows * heads * lanes, chunk * prefix_rows * heads, 8_000_000),
             )(flag, q, acc, prefix)
         )
@@ -553,7 +551,7 @@
     for c in range(CHUNKS):
         far = across(attended[c], 2)
         core = across(attended[c], 1)
-        both = across(attended[c], 3)
+        both = across(far, 1) if c == 0 else across(attended[c], 3)
         operands = [lengths, rank, attended[c], core, far, both, w_out, w_core, w_far, w_both, rows, step_rates.reshape(1, width)]
         specs = [SMEM] * 2 + [VMEM] * 8 + [pl.BlockSpec((chunk, width), lambda i, c=c: (c, 0)), VMEM]
         aliases = {}

time: 153 us -> 160 us (1.046)
  the two profiles are of different devices: /device:TPU:1 before, /device:TPU:25 now
where the time goes in v2:
time: 160 us; the launch traced here: 159 us
  Pallas kernels  59.1 us (37%)
  waiting for transfers between devices  48.7 us (30%)
  starting transfers between devices  38.3 us (24%)
  local copies, waits for them, and re-layouts  10.4 us (6%)
  between operations  2.29 us (1%)
    ppermute x16, starting transfers between devices, fetch(): return lax.ppermute(array, 'req', pairs)  27.5 us
    ppermute x9, waiting for transfers between devices, across(): return lax.ppermute(array, 'tp', [(i, i ^ bit) for i in range(4)])  25.8 us
    pallas_call x2, Pallas kernels, local(): pl.pallas_call(lambda *refs: attend_kernel(*refs, tile=1024), grid=(1,),...  23.8 us
    ppermute x16, waiting for transfers between devices, fetch(): return lax.ppermute(array, 'req', pairs)  22.9 us
    pallas_call x1, Pallas kernels, local(): pl.pallas_call(lambda *refs: suffix_kernel(*refs, tile=256), out_shape=sh...  16.5 us
    ppermute x9, starting transfers between devices, across(): return lax.ppermute(array, 'tp', [(i, i ^ bit) for i in range(4)])  10.8 us
    unnamed x48, local copies, waits for them, and re-layouts  10.4 us
    pallas_call x2, Pallas kernels, local(): pl.pallas_call(lambda *refs, c=c: output_kernel(*refs, tile=256, start=c...  8.34 us
  transfers between devices with their start and end apart: 25, of which 10 were waited for; matrix products, arithmetic and copies ran while one was open for 0% of the time, Pallas kernels for 31%

profile of v2, /device:TPU:25, one launch (start us, length us, event | category | flops | bytes accessed | tf_op | source)
XLA Modules:
  0.0 159.0 jit_solution(14481430967601208789)
XLA Ops:
  0.7 1.7 %prep.1 = (s32[1]{0:T(128)}, bf16[6,64,128]{2,1,0:T(8,128)(2,1)}) custom-call(s32[1]{0:T(128)S(6)} %copy.17.member_ref.refs_0_, bf16[5,64,128]{2,1,0:T(8,128)(2,1)} %bitcast.17, f32[5,64]{1,0:T(8,128)} %refs_4_.1), custom_call_target="tpu_custom_call" | custom-call | bytes 300000 | tf_op jit(solution)/shard_map/prep/pallas_call | solution.py:496
  2.3 1.3 collective-permute-start.7
  3.6 6.9 %collective-permute-start.8 = (bf16[6,64,128]{2,1,0:T(8,128)(2,1)}, bf16[6,64,128]{2,1,0:T(8,128)(2,1)S(1)}, u32[]{:S(2)}, u32[]{:S(2)}) collective-permute-start(bf16[6,64,128]{2,1,0:T(8,128)(2,1)} %get-tuple-element.129.a_ref), channel_id=1, source_target_pairs={{64,0},{68,4},{72,8},{76,12},{80,16},{84,20},{88,24},{92,28},{96,3... | collective-permute-start | bytes 294920 | tf_op jit(solution)/shard_map/ppermute | solution.py:34
  10.6 2.3 %collective-permute-done.8.c_ref = bf16[6,64,128]{2,1,0:T(8,128)(2,1)S(1)} collective-permute-done((bf16[6,64,128]{2,1,0:T(8,128)(2,1)}, bf16[6,64,128]{2,1,0:T(8,128)(2,1)S(1)}, u32[]{:S(2)}, u32[]{:S(2)}) %collective-permute-start.8) | collective-permute-done | bytes 98336 | tf_op jit(solution)/shard_map/ppermute | solution.py:34
  12.9 6.2 %collective-permute-done.9.d_ref = bf16[6,64,128]{2,1,0:T(8,128)(2,1)S(1)} collective-permute-done((bf16[6,64,128]{2,1,0:T(8,128)(2,1)}, bf16[6,64,128]{2,1,0:T(8,128)(2,1)S(1)}, u32[]{:S(2)}, u32[]{:S(2)}) %collective-permute-start.9) | collective-permute-done | bytes 98336 | tf_op jit(solution)/shard_map/ppermute | solution.py:34
  20.1 1.5 collective-permute-start.10
  22.3 1.8 %collective-permute-start.12 = (bf16[4,6,32,128]{3,2,1,0:T(8,128)(2,1)S(1)}, bf16[4,6,32,128]{3,2,1,0:T(8,128)(2,1)S(1)}, u32[]{:S(2)}, u32[]{:S(2)}) collective-permute-start(bf16[4,6,32,128]{3,2,1,0:T(8,128)(2,1)S(1)} %get-tuple-element.130.refs_2_), channel_id=1, source_target_pairs={{96,0},{100,4},{104,8},{108,12},{112,16},{116,20},{120,24},{124,28... | collective-permute-start | bytes 589832 | tf_op jit(solution)/shard_map/ppermute | solution.py:34
  24.6 2.2 %collective-permute-start.14 = (bf16[4,6,32,128]{3,2,1,0:T(8,128)(2,1)S(1)}, bf16[4,6,32,128]{3,2,1,0:T(8,128)(2,1)S(1)}, u32[]{:S(2)}, u32[]{:S(2)}) collective-permute-start(bf16[4,6,32,128]{3,2,1,0:T(8,128)(2,1)S(1)} %get-tuple-element.131.refs_6_), channel_id=1, source_target_pairs={{12,0},{0,4},{4,8},{8,12},{28,16},{16,20},{20,24},{24,28},{44,32},... | collective-permute-start | bytes 589832 | tf_op jit(solution)/shard_map/ppermute | solution.py:34
  28.2 2.8 %plan.1 = (s32[128]{0:T(128)S(1)}, s32[32]{0:T(128)S(1)}, s32[1]{0:T(128)}) custom-call(s32[1]{0:T(128)S(6)} %copy.17.member_ref.refs_0_, s32[1]{0:T(128)} %bitcast.6.place_ref, s32[4,16]{1,0:T(4,128)S(1)} %copy-done.8, s32[128]{0:T(128)S(1)} %copy-done.9), custom_call_target="tpu_custom_call" | custom-call | bytes 1000000 | tf_op jit(solution)/shard_map/plan/pallas_call | solution.py:413
  31.0 4.0 %collective-permute-done.12.refs_5_ = bf16[4,6,32,128]{3,2,1,0:T(8,128)(2,1)S(1)} collective-permute-done((bf16[4,6,32,128]{3,2,1,0:T(8,128)(2,1)S(1)}, bf16[4,6,32,128]{3,2,1,0:T(8,128)(2,1)S(1)}, u32[]{:S(2)}, u32[]{:S(2)}) %collective-permute-start.12) | collective-permute-done | bytes 196640 | tf_op jit(solution)/shard_map/ppermute | solution.py:34
  35.1 1.6 pack.3
  37.4 1.7 %collective-permute-start.22 = (bf16[4,5,32,128]{3,2,1,0:T(8,128)(2,1)S(1)}, bf16[4,5,32,128]{3,2,1,0:T(8,128)(2,1)S(1)}, u32[]{:S(2)}, u32[]{:S(2)}) collective-permute-start(bf16[4,5,32,128]{3,2,1,0:T(8,128)(2,1)S(1)} %get-tuple-element.140), channel_id=1, source_target_pairs={{96,0},{100,4},{104,8},{108,12},{112,16},{116,20},{120,24},{124,28... | collective-permute-start | bytes 491528 | tf_op jit(solution)/shard_map/ppermute | solution.py:34
  39.3 2.5 %collective-permute-start.17 = (bf16[8,5,32,128]{3,2,1,0:T(8,128)(2,1)S(1)}, bf16[8,5,32,128]{3,2,1,0:T(8,128)(2,1)S(1)}, u32[]{:S(2)}, u32[]{:S(2)}) collective-permute-start(bf16[8,5,32,128]{3,2,1,0:T(8,128)(2,1)S(1)} %get-tuple-element.134), channel_id=1, source_target_pairs={{12,0},{0,4},{4,8},{8,12},{28,16},{16,20},{20,24},{24,28},{44,32},... | collective-permute-start | bytes 983048 | tf_op jit(solution)/shard_map/ppermute | solution.py:34
  41.8 1.6 collective-permute-done.21
  43.4 7.4 %collective-permute-start.19 = (bf16[8,5,32,128]{3,2,1,0:T(8,128)(2,1)S(1)}, bf16[8,5,32,128]{3,2,1,0:T(8,128)(2,1)S(1)}, u32[]{:S(2)}, u32[]{:S(2)}) collective-permute-start(bf16[8,5,32,128]{3,2,1,0:T(8,128)(2,1)S(1)} %get-tuple-element.137), channel_id=1, source_target_pairs={{16,0},{20,4},{24,8},{28,12},{32,16},{36,20},{40,24},{44,28},{48,3... | collective-permute-start | bytes 983048 | tf_op jit(solution)/shard_map/ppermute | solution.py:34
  51.8 5.2 %collective-permute-done.19 = bf16[8,5,32,128]{3,2,1,0:T(8,128)(2,1)S(1)} collective-permute-done((bf16[8,5,32,128]{3,2,1,0:T(8,128)(2,1)S(1)}, bf16[8,5,32,128]{3,2,1,0:T(8,128)(2,1)S(1)}, u32[]{:S(2)}, u32[]{:S(2)}) %collective-permute-start.19) | collective-permute-done | bytes 327712 | tf_op jit(solution)/shard_map/ppermute | solution.py:34
  57.1 3.1 %collective-permute-done.20 = bf16[8,5,32,128]{3,2,1,0:T(8,128)(2,1)S(1)} collective-permute-done((bf16[8,5,32,128]{3,2,1,0:T(8,128)(2,1)S(1)}, bf16[8,5,32,128]{3,2,1,0:T(8,128)(2,1)S(1)}, u32[]{:S(2)}, u32[]{:S(2)}) %collective-permute-start.20) | collective-permute-done | bytes 327712 | tf_op jit(solution)/shard_map/ppermute | solution.py:34
  60.3 2.6 %conditional.1 = (bf16[5,1024,128]{2,1,0:T(8,128)(2,1)S(1)}) conditional(s32[]{:T(128)} %bitcast.7, (s32[32]{0:T(128)S(1)}, bf16[16,5,32,128]{3,2,1,0:T(8,128)(2,1)S(1)}, bf16[8,5,32,128]{3,2,1,0:T(8,128)(2,1)S(1)}, bf16[8,5,32,128]{3,2,1,0:T(8,128)(2,1)S(1)}, bf16[8,5,32,128]{3,2,1,0:T(8,128)(2,1)S(1)}, ...), branch_computations={%region_0.0_spmd, %region_1.0_spmd} | conditional | bytes 14864608 | solution.py:470
  60.3 2.4 %select.2 = bf16[5,1024,128]{2,1,0:T(8,128)(2,1)S(1)} custom-call(s32[32]{0:T(128)S(1)} %get-tuple-element.68.recv_ref, bf16[16,5,32,128]{3,2,1,0:T(8,128)(2,1)S(1)} %get-tuple-element.69.rest_0_, bf16[8,5,32,128]{3,2,1,0:T(8,128)(2,1)S(1)} %get-tuple-element.70.rest_1_, bf16[8,5,32,128]{3,2,1,0:T(8,128)(2,1)S(1)} %get-tuple-element.71.rest_2_, ...), custom_call_target="tpu_custom_call" | custom-call | bytes 3000000 | tf_op jit(solution)/shard_map/cond/branch_0_fun/select/pallas_call | solution.py:458
  64.0 3.0 %collective-permute-start.26 = (bf16[320,1280]{1,0:T(8,128)(2,1)S(1)}, bf16[320,1280]{1,0:T(8,128)(2,1)S(1)}, u32[]{:S(2)}, u32[]{:S(2)}) collective-permute-start(bf16[320,1280]{1,0:T(8,128)(2,1)S(1)} %copy-done.1), channel_id=1, source_target_pairs={{0,1},{1,0},{2,3},{3,2},{4,5},{5,4},{6,7},{7,6},{8,9},{9,8},{10,11... | collective-permute-start | bytes 2457608 | tf_op jit(solution)/shard_map/ppermute | solution.py:393
  67.0 16.3 %collective-permute-done.27.refs_8_ = bf16[320,1280]{1,0:T(8,128)(2,1)S(1)} collective-permute-done((bf16[320,1280]{1,0:T(8,128)(2,1)S(1)}, bf16[320,1280]{1,0:T(8,128)(2,1)S(1)}, u32[]{:S(2)}, u32[]{:S(2)}) %collective-permute-start.27) | collective-permute-done | bytes 819232 | tf_op jit(solution)/shard_map/ppermute | solution.py:393
  83.3 2.8 %collective-permute-start.28 = (bf16[320,1280]{1,0:T(8,128)(2,1)S(1)}, bf16[320,1280]{1,0:T(8,128)(2,1)}, u32[]{:S(2)}, u32[]{:S(2)}) collective-permute-start(bf16[320,1280]{1,0:T(8,128)(2,1)S(1)} %collective-permute-done.27.refs_8_), channel_id=1, source_target_pairs={{0,1},{1,0},{2,3},{3,2},{4,5},{5,4},{6,7},{7,6},{8,9},{9,8},{10,11... | collective-permute-start | bytes 2457608 | tf_op jit(solution)/shard_map/ppermute | solution.py:393
  88.0 1.1 copy-done.11
  90.3 2.0 %qkv.1 = (bf16[5,512,128]{2,1,0:T(8,128)(2,1)S(1)}, bf16[5,512,128]{2,1,0:T(8,128)(2,1)S(1)}) custom-call(bf16[512,1280]{1,0:T(8,128)(2,1)S(1)} %bitcast.11, bf16[320,1280]{1,0:T(8,128)(2,1)S(1)} %bitcast.14, bf16[320,1280]{1,0:T(8,128)(2,1)S(1)} %bitcast.15, bf16[320,1280]{1,0:T(8,128)(2,1)S(1)} %bitcast.16, f32[5,64]{1,0:T(8,128)S(1)} %copy-done.7), custom_call_target="tpu_custom_call" | custom-call | flops 1258291200 | bytes 10000000 | tf_op jit(solution)/shard_map/qkv/pallas_call | solution.py:506
  92.3 16.5 %suffix.1.refs_2_ = f32[5,512,128]{2,1,0:T(8,128)S(1)} custom-call(s32[1]{0:T(128)S(6)} %copy.18.refs_0_, s32[1]{0:T(128)} %get-tuple-element.123.refs_1_.refs_0_, bf16[5,512,128]{2,1,0:T(8,128)(2,1)S(1)} %get-tuple-element.124.refs_2_.refs_1_, bf16[5,512,128]{2,1,0:T(8,128)(2,1)S(1)} %get-tuple-element.125.refs_3_), custom_call_target="tpu_custom_call" | custom-call | flops 671088640 | bytes 10000000 | tf_op jit(solution)/shard_map/suffix/pallas_call | solution.py:516
  108.8 11.9 %shard_map.119.refs_2_ = bf16[256,320]{1,0:T(8,128)(2,1)S(1)} custom-call(s32[1]{0:T(128)} %get-tuple-element.123.refs_1_.refs_0_, bf16[5,512,128]{2,1,0:T(8,128)(2,1)S(1)} %get-tuple-element.124.refs_2_.refs_1_, f32[5,512,128]{2,1,0:T(8,128)S(1)} %suffix.1.refs_2_, bf16[5,1024,128]{2,1,0:T(8,128)(2,1)S(1)} %copy-done.14), custom_call_target="tpu_custom_call" | custom-call | flops 671088640 | bytes 8000000 | tf_op jit(solution)/shard_map/pallas_call | solution.py:534
  121.1 7.7 %collective-permute-done.30.refs_4_ = bf16[256,320]{1,0:T(8,128)(2,1)S(1)} collective-permute-done((bf16[256,320]{1,0:T(8,128)(2,1)S(1)}, bf16[256,320]{1,0:T(8,128)(2,1)S(1)}, u32[]{:S(2)}, u32[]{:S(2)}) %collective-permute-start.30) | collective-permute-done | bytes 163872 | tf_op jit(solution)/shard_map/ppermute | solution.py:393
  129.6 11.9 %shard_map.118.refs_2_ = bf16[256,320]{1,0:T(8,128)(2,1)S(1)} custom-call(s32[1]{0:T(128)} %get-tuple-element.123.refs_1_.refs_0_, bf16[5,512,128]{2,1,0:T(8,128)(2,1)S(1)} %get-tuple-element.124.refs_2_.refs_1_, f32[5,512,128]{2,1,0:T(8,128)S(1)} %suffix.1.refs_2_, bf16[5,1024,128]{2,1,0:T(8,128)(2,1)S(1)} %copy-done.14), custom_call_target="tpu_custom_call" | custom-call | flops 671088640 | bytes 8000000 | tf_op jit(solution)/shard_map/pallas_call | solution.py:534
  143.2 3.6 %collective-permute-start.25 = (bf16[256,320]{1,0:T(8,128)(2,1)S(1)}, bf16[256,320]{1,0:T(8,128)(2,1)}, u32[]{:S(2)}, u32[]{:S(2)}) collective-permute-start(bf16[256,320]{1,0:T(8,128)(2,1)S(1)} %shard_map.118.refs_2_), channel_id=1, source_target_pairs={{0,3},{1,2},{2,1},{3,0},{4,7},{5,6},{6,5},{7,4},{8,11},{9,10},{10,... | collective-permute-start | bytes 491528 | tf_op jit(solution)/shard_map/ppermute | solution.py:393
  149.0 4.1 %output.2.refs_12_ = bf16[320,512]{1,0:T(8,128)(2,1)} custom-call(s32[1]{0:T(128)S(6)} %copy.18.refs_0_, s32[1]{0:T(128)} %bitcast.refs_1_, bf16[256,320]{1,0:T(8,128)(2,1)S(1)} %shard_map.119.refs_2_, bf16[256,320]{1,0:T(8,128)(2,1)S(1)} %copy-done.5, bf16[256,320]{1,0:T(8,128)(2,1)S(1)} %collective-permute-done.30.refs_4_, ...), custom_call_target="tpu_custom_call" | custom-call | flops 838860800 | bytes 6000000 | tf_op jit(solution)/shard_map/output/pallas_call | solution.py:562
  153.0 1.7 %collective-permute-done.25.refs_5_ = bf16[256,320]{1,0:T(8,128)(2,1)} collective-permute-done((bf16[256,320]{1,0:T(8,128)(2,1)S(1)}, bf16[256,320]{1,0:T(8,128)(2,1)}, u32[]{:S(2)}, u32[]{:S(2)}) %collective-permute-start.25) | collective-permute-done | bytes 163872 | tf_op jit(solution)/shard_map/ppermute | solution.py:393
  154.8 4.3 %output.3 = bf16[320,512]{1,0:T(8,128)(2,1)} custom-call(s32[1]{0:T(128)S(6)} %copy.18.refs_0_, s32[1]{0:T(128)} %bitcast.refs_1_, bf16[256,320]{1,0:T(8,128)(2,1)S(1)} %shard_map.118.refs_2_, bf16[256,320]{1,0:T(8,128)(2,1)} %collective-permute-done.23.refs_3_, bf16[256,320]{1,0:T(8,128)(2,1)} %collective-permute-done.24.refs_4_, ...), custom_call_target="tpu_custom_call", output_to_operand_aliasing={{}: (12, {})} | custom-call | flops 838860800 | bytes 6000000 | tf_op jit(solution)/shard_map/output/pallas_call | solution.py:562
  (79 shorter events, 13.1 us)
Async XLA Ops:
  2.3 8.2 %collective-permute-start.7 = (bf16[6,64,128]{2,1,0:T(8,128)(2,1)}, bf16[6,64,128]{2,1,0:T(8,128)(2,1)S(1)}, u32[]{:S(2)}, u32[]{:S(2)}) collective-permute-start(bf16[6,64,128]{2,1,0:T(8,128)(2,1)} %get-tuple-element.129.a_ref), channel_id=1, source_target_pairs={{128,0},{132,4},{136,8},{140,12},{144,16},{148,20},{152,24},{156,2... | collective-permute-start | bytes 294920 | tf_op jit(solution)/shard_map/ppermute | solution.py:34
  3.6 9.3 %collective-permute-start.8 = (bf16[6,64,128]{2,1,0:T(8,128)(2,1)}, bf16[6,64,128]{2,1,0:T(8,128)(2,1)S(1)}, u32[]{:S(2)}, u32[]{:S(2)}) collective-permute-start(bf16[6,64,128]{2,1,0:T(8,128)(2,1)} %get-tuple-element.129.a_ref), channel_id=1, source_target_pairs={{64,0},{68,4},{72,8},{76,12},{80,16},{84,20},{88,24},{92,28},{96,3... | collective-permute-start | bytes 294920 | tf_op jit(solution)/shard_map/ppermute | solution.py:34
  10.5 8.6 %collective-permute-start.9 = (bf16[6,64,128]{2,1,0:T(8,128)(2,1)}, bf16[6,64,128]{2,1,0:T(8,128)(2,1)S(1)}, u32[]{:S(2)}, u32[]{:S(2)}) collective-permute-start(bf16[6,64,128]{2,1,0:T(8,128)(2,1)} %get-tuple-element.129.a_ref), channel_id=1, source_target_pairs={{192,0},{196,4},{200,8},{204,12},{208,16},{212,20},{216,24},{220,2... | collective-permute-start | bytes 294920 | tf_op jit(solution)/shard_map/ppermute | solution.py:34
  20.1 40.1 %copy-start.15 = (bf16[4,6,32,128]{3,2,1,0:T(8,128)(2,1)}, bf16[4,6,32,128]{3,2,1,0:T(8,128)(2,1)S(1)}, u32[]{:S(2)}) copy-start(bf16[4,6,32,128]{3,2,1,0:T(8,128)(2,1)S(1)} %get-tuple-element.130.refs_2_) | copy-start | bytes 589828
  20.1 40.1 %copy-start.16 = (bf16[4,6,32,128]{3,2,1,0:T(8,128)(2,1)}, bf16[4,6,32,128]{3,2,1,0:T(8,128)(2,1)S(1)}, u32[]{:S(2)}) copy-start(bf16[4,6,32,128]{3,2,1,0:T(8,128)(2,1)S(1)} %get-tuple-element.131.refs_6_) | copy-start | bytes 589828
  20.1 6.7 %collective-permute-start.10 = (bf16[4,6,32,128]{3,2,1,0:T(8,128)(2,1)S(1)}, bf16[4,6,32,128]{3,2,1,0:T(8,128)(2,1)S(1)}, u32[]{:S(2)}, u32[]{:S(2)}) collective-permute-start(bf16[4,6,32,128]{3,2,1,0:T(8,128)(2,1)S(1)} %get-tuple-element.130.refs_2_), channel_id=1, source_target_pairs={{16,0},{20,4},{24,8},{28,12},{32,16},{36,20},{40,24},{44,28},{48,3... | collective-permute-start | bytes 589832 | tf_op jit(solution)/shard_map/ppermute | solution.py:34
  21.6 9.4 %collective-permute-start.11 = (bf16[4,6,32,128]{3,2,1,0:T(8,128)(2,1)S(1)}, bf16[4,6,32,128]{3,2,1,0:T(8,128)(2,1)S(1)}, u32[]{:S(2)}, u32[]{:S(2)}) collective-permute-start(bf16[4,6,32,128]{3,2,1,0:T(8,128)(2,1)S(1)} %get-tuple-element.130.refs_2_), channel_id=1, source_target_pairs={{112,0},{116,4},{120,8},{124,12},{0,16},{4,20},{8,24},{12,28},{16,... | collective-permute-start | bytes 589832 | tf_op jit(solution)/shard_map/ppermute | solution.py:34
  22.3 12.8 %collective-permute-start.12 = (bf16[4,6,32,128]{3,2,1,0:T(8,128)(2,1)S(1)}, bf16[4,6,32,128]{3,2,1,0:T(8,128)(2,1)S(1)}, u32[]{:S(2)}, u32[]{:S(2)}) collective-permute-start(bf16[4,6,32,128]{3,2,1,0:T(8,128)(2,1)S(1)} %get-tuple-element.130.refs_2_), channel_id=1, source_target_pairs={{96,0},{100,4},{104,8},{108,12},{112,16},{116,20},{120,24},{124,28... | collective-permute-start | bytes 589832 | tf_op jit(solution)/shard_map/ppermute | solution.py:34
  24.1 11.0 %collective-permute-start.13 = (bf16[4,6,32,128]{3,2,1,0:T(8,128)(2,1)S(1)}, bf16[4,6,32,128]{3,2,1,0:T(8,128)(2,1)S(1)}, u32[]{:S(2)}, u32[]{:S(2)}) collective-permute-start(bf16[4,6,32,128]{3,2,1,0:T(8,128)(2,1)S(1)} %get-tuple-element.131.refs_6_), channel_id=1, source_target_pairs={{4,0},{8,4},{12,8},{0,12},{20,16},{24,20},{28,24},{16,28},{36,32},... | collective-permute-start | bytes 589832 | tf_op jit(solution)/shard_map/ppermute | solution.py:34
  24.6 10.5 %collective-permute-start.14 = (bf16[4,6,32,128]{3,2,1,0:T(8,128)(2,1)S(1)}, bf16[4,6,32,128]{3,2,1,0:T(8,128)(2,1)S(1)}, u32[]{:S(2)}, u32[]{:S(2)}) collective-permute-start(bf16[4,6,32,128]{3,2,1,0:T(8,128)(2,1)S(1)} %get-tuple-element.131.refs_6_), channel_id=1, source_target_pairs={{12,0},{0,4},{4,8},{8,12},{28,16},{16,20},{20,24},{24,28},{44,32},... | collective-permute-start | bytes 589832 | tf_op jit(solution)/shard_map/ppermute | solution.py:34
  26.8 33.4 %copy-start.17 = (bf16[4,6,32,128]{3,2,1,0:T(8,128)(2,1)}, bf16[4,6,32,128]{3,2,1,0:T(8,128)(2,1)S(1)}, u32[]{:S(2)}) copy-start(bf16[4,6,32,128]{3,2,1,0:T(8,128)(2,1)S(1)} %collective-permute-done.10.refs_3_) | copy-start | bytes 589828
  26.8 8.3 %collective-permute-start.15 = (bf16[4,6,32,128]{3,2,1,0:T(8,128)(2,1)S(1)}, bf16[4,6,32,128]{3,2,1,0:T(8,128)(2,1)S(1)}, u32[]{:S(2)}, u32[]{:S(2)}) collective-permute-start(bf16[4,6,32,128]{3,2,1,0:T(8,128)(2,1)S(1)} %get-tuple-element.131.refs_6_), channel_id=1, source_target_pairs={{8,0},{12,4},{0,8},{4,12},{24,16},{28,20},{16,24},{20,28},{40,32},... | collective-permute-start | bytes 589832 | tf_op jit(solution)/shard_map/ppermute | solution.py:34
  31.0 29.2 %copy-start.18 = (bf16[4,6,32,128]{3,2,1,0:T(8,128)(2,1)}, bf16[4,6,32,128]{3,2,1,0:T(8,128)(2,1)S(1)}, u32[]{:S(2)}) copy-start(bf16[4,6,32,128]{3,2,1,0:T(8,128)(2,1)S(1)} %collective-permute-done.11.refs_4_) | copy-start | bytes 589828
  36.7 6.7 %collective-permute-start.21 = (bf16[4,5,32,128]{3,2,1,0:T(8,128)(2,1)S(1)}, bf16[4,5,32,128]{3,2,1,0:T(8,128)(2,1)S(1)}, u32[]{:S(2)}, u32[]{:S(2)}) collective-permute-start(bf16[4,5,32,128]{3,2,1,0:T(8,128)(2,1)S(1)} %get-tuple-element.139), channel_id=1, source_target_pairs={{32,0},{36,4},{40,8},{44,12},{48,16},{52,20},{56,24},{60,28},{64,3... | collective-permute-start | bytes 491528 | tf_op jit(solution)/shard_map/ppermute | solution.py:34
  37.4 13.4 %collective-permute-start.22 = (bf16[4,5,32,128]{3,2,1,0:T(8,128)(2,1)S(1)}, bf16[4,5,32,128]{3,2,1,0:T(8,128)(2,1)S(1)}, u32[]{:S(2)}, u32[]{:S(2)}) collective-permute-start(bf16[4,5,32,128]{3,2,1,0:T(8,128)(2,1)S(1)} %get-tuple-element.140), channel_id=1, source_target_pairs={{96,0},{100,4},{104,8},{108,12},{112,16},{116,20},{120,24},{124,28... | collective-permute-start | bytes 491528 | tf_op jit(solution)/shard_map/ppermute | solution.py:34
  39.1 12.3 %collective-permute-start.16 = (bf16[8,5,32,128]{3,2,1,0:T(8,128)(2,1)S(1)}, bf16[8,5,32,128]{3,2,1,0:T(8,128)(2,1)S(1)}, u32[]{:S(2)}, u32[]{:S(2)}) collective-permute-start(bf16[8,5,32,128]{3,2,1,0:T(8,128)(2,1)S(1)} %get-tuple-element.133), channel_id=1, source_target_pairs={{4,0},{8,4},{12,8},{0,12},{20,16},{24,20},{28,24},{16,28},{36,32},... | collective-permute-start | bytes 983048 | tf_op jit(solution)/shard_map/ppermute | solution.py:34
  39.3 12.1 %collective-permute-start.17 = (bf16[8,5,32,128]{3,2,1,0:T(8,128)(2,1)S(1)}, bf16[8,5,32,128]{3,2,1,0:T(8,128)(2,1)S(1)}, u32[]{:S(2)}, u32[]{:S(2)}) collective-permute-start(bf16[8,5,32,128]{3,2,1,0:T(8,128)(2,1)S(1)} %get-tuple-element.134), channel_id=1, source_target_pairs={{12,0},{0,4},{4,8},{8,12},{28,16},{16,20},{20,24},{24,28},{44,32},... | collective-permute-start | bytes 983048 | tf_op jit(solution)/shard_map/ppermute | solution.py:34
  41.8 10.0 %collective-permute-start.18 = (bf16[8,5,32,128]{3,2,1,0:T(8,128)(2,1)S(1)}, bf16[8,5,32,128]{3,2,1,0:T(8,128)(2,1)S(1)}, u32[]{:S(2)}, u32[]{:S(2)}) collective-permute-start(bf16[8,5,32,128]{3,2,1,0:T(8,128)(2,1)S(1)} %get-tuple-element.135), channel_id=1, source_target_pairs={{8,0},{12,4},{0,8},{4,12},{24,16},{28,20},{16,24},{20,28},{40,32},... | collective-permute-start | bytes 983048 | tf_op jit(solution)/shard_map/ppermute | solution.py:34
  43.4 13.7 %collective-permute-start.19 = (bf16[8,5,32,128]{3,2,1,0:T(8,128)(2,1)S(1)}, bf16[8,5,32,128]{3,2,1,0:T(8,128)(2,1)S(1)}, u32[]{:S(2)}, u32[]{:S(2)}) collective-permute-start(bf16[8,5,32,128]{3,2,1,0:T(8,128)(2,1)S(1)} %get-tuple-element.137), channel_id=1, source_target_pairs={{16,0},{20,4},{24,8},{28,12},{32,16},{36,20},{40,24},{44,28},{48,3... | collective-permute-start | bytes 983048 | tf_op jit(solution)/shard_map/ppermute | solution.py:34
  50.8 9.4 %collective-permute-start.20 = (bf16[8,5,32,128]{3,2,1,0:T(8,128)(2,1)S(1)}, bf16[8,5,32,128]{3,2,1,0:T(8,128)(2,1)S(1)}, u32[]{:S(2)}, u32[]{:S(2)}) collective-permute-start(bf16[8,5,32,128]{3,2,1,0:T(8,128)(2,1)S(1)} %get-tuple-element.138), channel_id=1, source_target_pairs={{112,0},{116,4},{120,8},{124,12},{0,16},{4,20},{8,24},{12,28},{16,... | collective-permute-start | bytes 983048 | tf_op jit(solution)/shard_map/ppermute | solution.py:34
  60.3 26.5 %copy-start = (bf16[1,512,1280]{2,1,0:T(8,128)(2,1)S(1)}, bf16[1,512,1280]{2,1,0:T(8,128)(2,1)}, u32[]{:S(2)}) copy-start(bf16[1,512,1280]{2,1,0:T(8,128)(2,1)} %param.14) | copy-start | bytes 3932164
  60.3 26.5 %copy-start.7 = (f32[5,64]{1,0:T(8,128)S(1)}, f32[5,64]{1,0:T(8,128)}, u32[]{:S(2)}) copy-start(f32[5,64]{1,0:T(8,128)} %refs_4_.1) | copy-start | bytes 3844
  64.0 19.3 %collective-permute-start.27 = (bf16[320,1280]{1,0:T(8,128)(2,1)S(1)}, bf16[320,1280]{1,0:T(8,128)(2,1)S(1)}, u32[]{:S(2)}, u32[]{:S(2)}) collective-permute-start(bf16[320,1280]{1,0:T(8,128)(2,1)S(1)} %copy-done.1), channel_id=1, source_target_pairs={{0,2},{1,3},{2,0},{3,1},{4,6},{5,7},{6,4},{7,5},{8,10},{9,11},{10,... | collective-permute-start | bytes 2457608 | tf_op jit(solution)/shard_map/ppermute | solution.py:393
  64.0 78.4 %collective-permute-start.26 = (bf16[320,1280]{1,0:T(8,128)(2,1)S(1)}, bf16[320,1280]{1,0:T(8,128)(2,1)S(1)}, u32[]{:S(2)}, u32[]{:S(2)}) collective-permute-start(bf16[320,1280]{1,0:T(8,128)(2,1)S(1)} %copy-done.1), channel_id=1, source_target_pairs={{0,1},{1,0},{2,3},{3,2},{4,5},{5,4},{6,7},{7,6},{8,9},{9,8},{10,11... | collective-permute-start | bytes 2457608 | tf_op jit(solution)/shard_map/ppermute | solution.py:393
  83.3 63.5 %collective-permute-start.28 = (bf16[320,1280]{1,0:T(8,128)(2,1)S(1)}, bf16[320,1280]{1,0:T(8,128)(2,1)}, u32[]{:S(2)}, u32[]{:S(2)}) collective-permute-start(bf16[320,1280]{1,0:T(8,128)(2,1)S(1)} %collective-permute-done.27.refs_8_), channel_id=1, source_target_pairs={{0,1},{1,0},{2,3},{3,2},{4,5},{5,4},{6,7},{7,6},{8,9},{9,8},{10,11... | collective-permute-start | bytes 2457608 | tf_op jit(solution)/shard_map/ppermute | solution.py:393
  120.7 26.1 %copy-start.23 = (f32[1280]{0:T(1024)S(1)}, f32[1280]{0:T(1024)}, u32[]{:S(2)}) copy-start(f32[1280]{0:T(1024)} %param.24) | copy-start | bytes 15364
  120.7 8.1 %collective-permute-start.30 = (bf16[256,320]{1,0:T(8,128)(2,1)S(1)}, bf16[256,320]{1,0:T(8,128)(2,1)S(1)}, u32[]{:S(2)}, u32[]{:S(2)}) collective-permute-start(bf16[256,320]{1,0:T(8,128)(2,1)S(1)} %shard_map.119.refs_2_), channel_id=1, source_target_pairs={{0,2},{1,3},{2,0},{3,1},{4,6},{5,7},{6,4},{7,5},{8,10},{9,11},{10,... | collective-permute-start | bytes 491528 | tf_op jit(solution)/shard_map/ppermute | solution.py:393
  120.8 20.8 %collective-permute-start.29 = (bf16[256,320]{1,0:T(8,128)(2,1)S(1)}, bf16[256,320]{1,0:T(8,128)(2,1)S(1)}, u32[]{:S(2)}, u32[]{:S(2)}) collective-permute-start(bf16[256,320]{1,0:T(8,128)(2,1)S(1)} %shard_map.119.refs_2_), channel_id=1, source_target_pairs={{0,1},{1,0},{2,3},{3,2},{4,5},{5,4},{6,7},{7,6},{8,9},{9,8},{10,11... | collective-permute-start | bytes 491528 | tf_op jit(solution)/shard_map/ppermute | solution.py:393
  128.8 18.1 %collective-permute-start.31 = (bf16[256,320]{1,0:T(8,128)(2,1)S(1)}, bf16[256,320]{1,0:T(8,128)(2,1)}, u32[]{:S(2)}, u32[]{:S(2)}) collective-permute-start(bf16[256,320]{1,0:T(8,128)(2,1)S(1)} %collective-permute-done.30.refs_4_), channel_id=1, source_target_pairs={{0,1},{1,0},{2,3},{3,2},{4,5},{5,4},{6,7},{7,6},{8,9},{9,8},{10,11... | collective-permute-start | bytes 491528 | tf_op jit(solution)/shard_map/ppermute | solution.py:393
  141.5 11.5 %collective-permute-start.23 = (bf16[256,320]{1,0:T(8,128)(2,1)S(1)}, bf16[256,320]{1,0:T(8,128)(2,1)}, u32[]{:S(2)}, u32[]{:S(2)}) collective-permute-start(bf16[256,320]{1,0:T(8,128)(2,1)S(1)} %shard_map.118.refs_2_), channel_id=1, source_target_pairs={{0,1},{1,0},{2,3},{3,2},{4,5},{5,4},{6,7},{7,6},{8,9},{9,8},{10,11... | collective-permute-start | bytes 491528 | tf_op jit(solution)/shard_map/ppermute | solution.py:393
  142.3 10.7 %collective-permute-start.24 = (bf16[256,320]{1,0:T(8,128)(2,1)S(1)}, bf16[256,320]{1,0:T(8,128)(2,1)}, u32[]{:S(2)}, u32[]{:S(2)}) collective-permute-start(bf16[256,320]{1,0:T(8,128)(2,1)S(1)} %shard_map.118.refs_2_), channel_id=1, source_target_pairs={{0,2},{1,3},{2,0},{3,1},{4,6},{5,7},{6,4},{7,5},{8,10},{9,11},{10,... | collective-permute-start | bytes 491528 | tf_op jit(solution)/shard_map/ppermute | solution.py:393
  143.2 11.5 %collective-permute-start.25 = (bf16[256,320]{1,0:T(8,128)(2,1)S(1)}, bf16[256,320]{1,0:T(8,128)(2,1)}, u32[]{:S(2)}, u32[]{:S(2)}) collective-permute-start(bf16[256,320]{1,0:T(8,128)(2,1)S(1)} %shard_map.118.refs_2_), channel_id=1, source_target_pairs={{0,3},{1,2},{2,1},{3,0},{4,7},{5,6},{6,5},{7,4},{8,11},{9,10},{10,... | collective-permute-start | bytes 491528 | tf_op jit(solution)/shard_map/ppermute | solution.py:393
  (17 other events, 131.2 us)

commit v3 on v2

--- a/solution.py
+++ b/solution.py
@@ -177,10 +177,12 @@
         lax.fori_loop(0, heads * pieces, piece, 0)
 
 
-def split_kernel(a_ref, b_ref, c_ref, d_ref, one_ref, two_ref):
+def split_kernel(a_ref, b_ref, c_ref, d_ref, one_ref, two_ref, pair_ref):
     rows = one_ref.shape[2]
     for n, ref in enumerate((a_ref, b_ref, c_ref, d_ref)):
         one_ref[n] = ref[:, :rows]
+        if n < 2:
+            pair_ref[n] = ref[:, :rows]
         two_ref[n] = ref[:, rows:]
 
 
@@ -232,15 +234,19 @@
 
 
 def pack_kernel(member_ref, send_ref, *rest, start):
-    quads, outs, pool_ref = (rest[:4], rest[4:8]), rest[8:-1], rest[-1]
+    pieces, outs, pool_ref = (rest[:5], rest[5:9]), rest[9:-1], rest[-1]
     heads = pool_ref.shape[2]
+    blocks = []
     for half in range(2):
-        for n in range(4):
-            pool_ref[half, 4 * n : 4 * n + 4] = quads[half][n][:, :heads]
+        held = [(ref, b) for ref in pieces[half] for b in range(ref.shape[0])]
+        blocks.append(held)
+        for n, (ref, b) in enumerate(held):
+            pool_ref[half, n] = ref[b, :heads]
 
     def wanted(target):
         n, k, b = member_spot(target)
-        value = quads[n][k][b, heads].astype(F32)
+        ref, b = blocks[n][4 * k + b]
+        value = ref[b, heads].astype(F32)
         return jnp.max(value).astype(jnp.int32)
 
     jobs = []
@@ -420,18 +426,24 @@
         compiler_params=vmem(1),
         cost_estimate=cost(0, 0, 1_000_000),
     )(membership, place, owners, table)
-    quads = pl.pallas_call(
+    *quads, pair = pl.pallas_call(
         split_kernel,
-        out_shape=(shaped((4, planes, part, lanes), BF16),) * 2,
+        out_shape=tuple(shaped((n, planes, part, lanes), BF16) for n in (4, 4, 2)),
         in_specs=[VMEM] * 4,
-        out_specs=(VMEM, VMEM),
+        out_specs=(VMEM,) * 3,
         name="split",
         compiler_params=vmem(2),
         cost_estimate=cost(0, 0, 600_000),
     )(whole, *[fetch(whole, offset) for offset in QUAD[1:]])
     held = []
-    for quad, half in zip(quads, HALVES):
-        held += [quad] + [fetch(quad, offset) for offset in half["pool"][1:]]
+    for n, (quad, half) in enumerate(zip(quads, HALVES)):
+        held.append(quad)
+        for i, offset in enumerate(half["pool"][1:]):
+            if n == 0 and i == 2:
+                held.append(fetch(pair, offset))
+                held.append(fetch(pair, add3(offset, QUAD[2])))
+            else:
+                held.append(fetch(quad, offset))
 
     def one_round(start):
         shapes, offsets = [], []
@@ -445,7 +457,7 @@
         packed = pl.pallas_call(
             lambda *refs: pack_kernel(*refs, start=start),
             out_shape=tuple(shaped((n, heads, part, lanes), BF16) for n in shapes),
-            in_specs=[SMEM] * 2 + [VMEM] * 8,
+            in_specs=[SMEM] * 2 + [VMEM] * 9,
             out_specs=(VMEM,) * len(shapes),
             scratch_shapes=[pltpu.VMEM((2, 16, heads, part, lanes), BF16)],
             name="pack",
@@ -551,7 +563,7 @@
     for c in range(CHUNKS):
         far = across(attended[c], 2)
         core = across(attended[c], 1)
-        both = across(far, 1) if c == 0 else across(attended[c], 3)
+        both = across(far, 1)
         operands = [lengths, rank, attended[c], core, far, both, w_out, w_core, w_far, w_both, rows, step_rates.reshape(1, width)]
         specs = [SMEM] * 2 + [VMEM] * 8 + [pl.BlockSpec((chunk, width), lambda i, c=c: (c, 0)), VMEM]
         aliases = {}
@@ -567,8 +579,7 @@
             out_specs=pl.BlockSpec((part, chunk), lambda i, c=c: (0, c)),
             input_output_aliases=aliases,
             scratch_shapes=[pltpu.VMEM((chunk, width), F32)],
-            name="output",
-        compiler_params=vmem(20),
+            compiler_params=vmem(20),
             cost_estimate=cost(2 * chunk * width * width, 0, 6_000_000),
         )(*operands)
     return out.T.reshape(1, suf, part)

time: 160 us -> 152 us (0.950)
  the two profiles are of different devices: /device:TPU:25 before, /device:TPU:1 now
where the time goes in v3:
time: 152 us; the launch traced here: 151 us
  Pallas kernels  59.8 us (39%)
  starting transfers between devices  49.6 us (33%)
  waiting for transfers between devices  31 us (20%)
  local copies, waits for them, and re-layouts  8.41 us (6%)
  between operations  2.25 us (1%)
    ppermute x17, starting transfers between devices, fetch(): return lax.ppermute(array, 'req', pairs)  26.4 us
    pallas_call x2, Pallas kernels, local(): pl.pallas_call(lambda *refs: attend_kernel(*refs, tile=1024), grid=(1,),...  24 us
    ppermute x9, starting transfers between devices, across(): return lax.ppermute(array, 'tp', [(i, i ^ bit) for i in range(4)])  23.2 us
    ppermute x17, waiting for transfers between devices, fetch(): return lax.ppermute(array, 'req', pairs)  20.9 us
    pallas_call x1, Pallas kernels, local(): pl.pallas_call(lambda *refs: suffix_kernel(*refs, tile=256), out_shape=sh...  16.5 us
    ppermute x9, waiting for transfers between devices, across(): return lax.ppermute(array, 'tp', [(i, i ^ bit) for i in range(4)])  10.1 us
    pallas_call x2, Pallas kernels, local(): pl.pallas_call(lambda *refs, c=c: output_kernel(*refs, tile=256, start=c...  8.82 us
    unnamed x44, local copies, waits for them, and re-layouts  8.4 us
  transfers between devices with their start and end apart: 26, of which 9 were waited for; matrix products, arithmetic and copies ran while one was open for 0% of the time, Pallas kernels for 33%

profile of v3, /device:TPU:1, one launch (start us, length us, event | category | flops | bytes accessed | tf_op | source)
XLA Modules:
  0.0 151.1 jit_solution(12970052338691147914)
XLA Ops:
  0.7 1.7 %prep.1 = (s32[1]{0:T(128)}, bf16[6,64,128]{2,1,0:T(8,128)(2,1)}) custom-call(s32[1]{0:T(128)S(6)} %copy.17.member_ref.refs_0_, bf16[5,64,128]{2,1,0:T(8,128)(2,1)} %bitcast.17, f32[5,64]{1,0:T(8,128)} %refs_4_.1), custom_call_target="tpu_custom_call" | custom-call | bytes 300000 | tf_op jit(solution)/shard_map/prep/pallas_call | solution.py:508
  2.3 2.1 %collective-permute-start.7 = (bf16[6,64,128]{2,1,0:T(8,128)(2,1)}, bf16[6,64,128]{2,1,0:T(8,128)(2,1)S(1)}, u32[]{:S(2)}, u32[]{:S(2)}) collective-permute-start(bf16[6,64,128]{2,1,0:T(8,128)(2,1)} %get-tuple-element.133.a_ref), channel_id=1, source_target_pairs={{128,0},{132,4},{136,8},{140,12},{144,16},{148,20},{152,24},{156,2... | collective-permute-start | bytes 294920 | tf_op jit(solution)/shard_map/ppermute | solution.py:34
  4.5 6.9 %collective-permute-start.8 = (bf16[6,64,128]{2,1,0:T(8,128)(2,1)}, bf16[6,64,128]{2,1,0:T(8,128)(2,1)S(1)}, u32[]{:S(2)}, u32[]{:S(2)}) collective-permute-start(bf16[6,64,128]{2,1,0:T(8,128)(2,1)} %get-tuple-element.133.a_ref), channel_id=1, source_target_pairs={{64,0},{68,4},{72,8},{76,12},{80,16},{84,20},{88,24},{92,28},{96,3... | collective-permute-start | bytes 294920 | tf_op jit(solution)/shard_map/ppermute | solution.py:34
  11.4 2.3 %collective-permute-done.8.c_ref = bf16[6,64,128]{2,1,0:T(8,128)(2,1)S(1)} collective-permute-done((bf16[6,64,128]{2,1,0:T(8,128)(2,1)}, bf16[6,64,128]{2,1,0:T(8,128)(2,1)S(1)}, u32[]{:S(2)}, u32[]{:S(2)}) %collective-permute-start.8) | collective-permute-done | bytes 98336 | tf_op jit(solution)/shard_map/ppermute | solution.py:34
  13.7 6.4 %collective-permute-done.9.d_ref = bf16[6,64,128]{2,1,0:T(8,128)(2,1)S(1)} collective-permute-done((bf16[6,64,128]{2,1,0:T(8,128)(2,1)}, bf16[6,64,128]{2,1,0:T(8,128)(2,1)S(1)}, u32[]{:S(2)}, u32[]{:S(2)}) %collective-permute-start.9) | collective-permute-done | bytes 98336 | tf_op jit(solution)/shard_map/ppermute | solution.py:34
  22.3 3.2 %collective-permute-start.13 = (bf16[2,6,32,128]{3,2,1,0:T(8,128)(2,1)S(1)}, bf16[2,6,32,128]{3,2,1,0:T(8,128)(2,1)S(1)}, u32[]{:S(2)}, u32[]{:S(2)}) collective-permute-start(bf16[2,6,32,128]{3,2,1,0:T(8,128)(2,1)S(1)} %get-tuple-element.135), channel_id=1, source_target_pairs={{32,0},{36,4},{40,8},{44,12},{48,16},{52,20},{56,24},{60,28},{64,3... | collective-permute-start | bytes 294920 | tf_op jit(solution)/shard_map/ppermute | solution.py:34
  25.5 2.7 %collective-permute-start.14 = (bf16[4,6,32,128]{3,2,1,0:T(8,128)(2,1)S(1)}, bf16[4,6,32,128]{3,2,1,0:T(8,128)(2,1)S(1)}, u32[]{:S(2)}, u32[]{:S(2)}) collective-permute-start(bf16[4,6,32,128]{3,2,1,0:T(8,128)(2,1)S(1)} %get-tuple-element.136.refs_7_), channel_id=1, source_target_pairs={{4,0},{8,4},{12,8},{0,12},{20,16},{24,20},{28,24},{16,28},{36,32},... | collective-permute-start | bytes 589832 | tf_op jit(solution)/shard_map/ppermute | solution.py:34
  28.2 1.6 %collective-permute-start.16 = (bf16[4,6,32,128]{3,2,1,0:T(8,128)(2,1)S(1)}, bf16[4,6,32,128]{3,2,1,0:T(8,128)(2,1)S(1)}, u32[]{:S(2)}, u32[]{:S(2)}) collective-permute-start(bf16[4,6,32,128]{3,2,1,0:T(8,128)(2,1)S(1)} %get-tuple-element.136.refs_7_), channel_id=1, source_target_pairs={{8,0},{12,4},{0,8},{4,12},{24,16},{28,20},{16,24},{20,28},{40,32},... | collective-permute-start | bytes 589832 | tf_op jit(solution)/shard_map/ppermute | solution.py:34
  32.7 2.8 %plan.1 = (s32[128]{0:T(128)S(1)}, s32[32]{0:T(128)S(1)}, s32[1]{0:T(128)}) custom-call(s32[1]{0:T(128)S(6)} %copy.17.member_ref.refs_0_, s32[1]{0:T(128)} %bitcast.6.place_ref, s32[4,16]{1,0:T(4,128)S(1)} %copy-done.6, s32[128]{0:T(128)S(1)} %copy-done.7), custom_call_target="tpu_custom_call" | custom-call | bytes 1000000 | tf_op jit(solution)/shard_map/plan/pallas_call | solution.py:419
  35.6 1.3 collective-permute-done.15.refs_9_
  36.9 1.6 %pack.3 = (bf16[16,5,32,128]{3,2,1,0:T(8,128)(2,1)S(1)}, bf16[8,5,32,128]{3,2,1,0:T(8,128)(2,1)S(1)}, bf16[8,5,32,128]{3,2,1,0:T(8,128)(2,1)S(1)}, bf16[8,5,32,1...) custom-call(s32[1]{0:T(128)S(6)} %copy.17.member_ref.refs_0_, ...), custom_call_target="tpu_custom_call" | custom-call | bytes 4000000 | tf_op jit(solution)/shard_map/pack/pallas_call | solution.py:457
  38.5 2.4 %collective-permute-start.22 = (bf16[4,5,32,128]{3,2,1,0:T(8,128)(2,1)S(1)}, bf16[4,5,32,128]{3,2,1,0:T(8,128)(2,1)S(1)}, u32[]{:S(2)}, u32[]{:S(2)}) collective-permute-start(bf16[4,5,32,128]{3,2,1,0:T(8,128)(2,1)S(1)} %get-tuple-element.144), channel_id=1, source_target_pairs={{32,0},{36,4},{40,8},{44,12},{48,16},{52,20},{56,24},{60,28},{64,3... | collective-permute-start | bytes 491528 | tf_op jit(solution)/shard_map/ppermute | solution.py:34
  40.9 1.2 collective-permute-start.17
  42.4 1.4 collective-permute-start.19
  44.7 1.9 %collective-permute-start.20 = (bf16[8,5,32,128]{3,2,1,0:T(8,128)(2,1)S(1)}, bf16[8,5,32,128]{3,2,1,0:T(8,128)(2,1)S(1)}, u32[]{:S(2)}, u32[]{:S(2)}) collective-permute-start(bf16[8,5,32,128]{3,2,1,0:T(8,128)(2,1)S(1)} %get-tuple-element.142), channel_id=1, source_target_pairs={{16,0},{20,4},{24,8},{28,12},{32,16},{36,20},{40,24},{44,28},{48,3... | collective-permute-start | bytes 983048 | tf_op jit(solution)/shard_map/ppermute | solution.py:34
  46.6 2.3 %collective-permute-done.23 = bf16[4,5,32,128]{3,2,1,0:T(8,128)(2,1)S(1)} collective-permute-done((bf16[4,5,32,128]{3,2,1,0:T(8,128)(2,1)S(1)}, bf16[4,5,32,128]{3,2,1,0:T(8,128)(2,1)S(1)}, u32[]{:S(2)}, u32[]{:S(2)}) %collective-permute-start.23) | collective-permute-done | bytes 163872 | tf_op jit(solution)/shard_map/ppermute | solution.py:34
  49.6 3.9 %collective-permute-done.18 = bf16[8,5,32,128]{3,2,1,0:T(8,128)(2,1)S(1)} collective-permute-done((bf16[8,5,32,128]{3,2,1,0:T(8,128)(2,1)S(1)}, bf16[8,5,32,128]{3,2,1,0:T(8,128)(2,1)S(1)}, u32[]{:S(2)}, u32[]{:S(2)}) %collective-permute-start.18) | collective-permute-done | bytes 327712 | tf_op jit(solution)/shard_map/ppermute | solution.py:34
  53.5 3.6 %collective-permute-done.21 = bf16[8,5,32,128]{3,2,1,0:T(8,128)(2,1)S(1)} collective-permute-done((bf16[8,5,32,128]{3,2,1,0:T(8,128)(2,1)S(1)}, bf16[8,5,32,128]{3,2,1,0:T(8,128)(2,1)S(1)}, u32[]{:S(2)}, u32[]{:S(2)}) %collective-permute-start.21) | collective-permute-done | bytes 327712 | tf_op jit(solution)/shard_map/ppermute | solution.py:34
  57.2 2.4 %conditional.1 = (bf16[5,1024,128]{2,1,0:T(8,128)(2,1)S(1)}) conditional(s32[]{:T(128)} %bitcast.7, (s32[32]{0:T(128)S(1)}, bf16[16,5,32,128]{3,2,1,0:T(8,128)(2,1)S(1)}, bf16[8,5,32,128]{3,2,1,0:T(8,128)(2,1)S(1)}, bf16[8,5,32,128]{3,2,1,0:T(8,128)(2,1)S(1)}, bf16[8,5,32,128]{3,2,1,0:T(8,128)(2,1)S(1)}, ...), branch_computations={%region_0.0_spmd, %region_1.0_spmd} | conditional | bytes 14864608 | solution.py:482
  57.2 2.4 %select.2 = bf16[5,1024,128]{2,1,0:T(8,128)(2,1)S(1)} custom-call(s32[32]{0:T(128)S(1)} %get-tuple-element.70.recv_ref, bf16[16,5,32,128]{3,2,1,0:T(8,128)(2,1)S(1)} %get-tuple-element.71.rest_0_, bf16[8,5,32,128]{3,2,1,0:T(8,128)(2,1)S(1)} %get-tuple-element.72.rest_1_, bf16[8,5,32,128]{3,2,1,0:T(8,128)(2,1)S(1)} %get-tuple-element.73.rest_2_, ...), custom_call_target="tpu_custom_call" | custom-call | bytes 3000000 | tf_op jit(solution)/shard_map/cond/branch_0_fun/select/pallas_call | solution.py:470
  60.7 2.5 %collective-permute-start.28 = (bf16[320,1280]{1,0:T(8,128)(2,1)S(1)}, bf16[320,1280]{1,0:T(8,128)(2,1)S(1)}, u32[]{:S(2)}, u32[]{:S(2)}) collective-permute-start(bf16[320,1280]{1,0:T(8,128)(2,1)S(1)} %copy-done.1), channel_id=1, source_target_pairs={{0,2},{1,3},{2,0},{3,1},{4,6},{5,7},{6,4},{7,5},{8,10},{9,11},{10,... | collective-permute-start | bytes 2457608 | tf_op jit(solution)/shard_map/ppermute | solution.py:399
  63.2 7.7 %collective-permute-start.27 = (bf16[320,1280]{1,0:T(8,128)(2,1)S(1)}, bf16[320,1280]{1,0:T(8,128)(2,1)}, u32[]{:S(2)}, u32[]{:S(2)}) collective-permute-start(bf16[320,1280]{1,0:T(8,128)(2,1)S(1)} %copy-done.1), channel_id=1, source_target_pairs={{0,1},{1,0},{2,3},{3,2},{4,5},{5,4},{6,7},{7,6},{8,9},{9,8},{10,11... | collective-permute-start | bytes 2457608 | tf_op jit(solution)/shard_map/ppermute | solution.py:399
  70.8 4.0 %collective-permute-done.28.refs_8_ = bf16[320,1280]{1,0:T(8,128)(2,1)S(1)} collective-permute-done((bf16[320,1280]{1,0:T(8,128)(2,1)S(1)}, bf16[320,1280]{1,0:T(8,128)(2,1)S(1)}, u32[]{:S(2)}, u32[]{:S(2)}) %collective-permute-start.28) | collective-permute-done | bytes 819232 | tf_op jit(solution)/shard_map/ppermute | solution.py:399
  74.8 8.0 %collective-permute-start.29 = (bf16[320,1280]{1,0:T(8,128)(2,1)S(1)}, bf16[320,1280]{1,0:T(8,128)(2,1)}, u32[]{:S(2)}, u32[]{:S(2)}) collective-permute-start(bf16[320,1280]{1,0:T(8,128)(2,1)S(1)} %collective-permute-done.28.refs_8_), channel_id=1, source_target_pairs={{0,1},{1,0},{2,3},{3,2},{4,5},{5,4},{6,7},{7,6},{8,9},{9,8},{10,11... | collective-permute-start | bytes 2457608 | tf_op jit(solution)/shard_map/ppermute | solution.py:399
  86.9 2.0 %qkv.1 = (bf16[5,512,128]{2,1,0:T(8,128)(2,1)S(1)}, bf16[5,512,128]{2,1,0:T(8,128)(2,1)S(1)}) custom-call(bf16[512,1280]{1,0:T(8,128)(2,1)S(1)} %bitcast.11, bf16[320,1280]{1,0:T(8,128)(2,1)S(1)} %bitcast.14, bf16[320,1280]{1,0:T(8,128)(2,1)S(1)} %bitcast.15, bf16[320,1280]{1,0:T(8,128)(2,1)S(1)} %bitcast.16, f32[5,64]{1,0:T(8,128)S(1)} %copy-done.5), custom_call_target="tpu_custom_call" | custom-call | flops 1258291200 | bytes 10000000 | tf_op jit(solution)/shard_map/qkv/pallas_call | solution.py:518
  89.0 16.5 %suffix.1.refs_2_ = f32[5,512,128]{2,1,0:T(8,128)S(1)} custom-call(s32[1]{0:T(128)S(6)} %copy.18.refs_0_, s32[1]{0:T(128)} %get-tuple-element.127.refs_1_.refs_0_, bf16[5,512,128]{2,1,0:T(8,128)(2,1)S(1)} %get-tuple-element.128.refs_2_.refs_1_, bf16[5,512,128]{2,1,0:T(8,128)(2,1)S(1)} %get-tuple-element.129.refs_3_), custom_call_target="tpu_custom_call" | custom-call | flops 671088640 | bytes 10000000 | tf_op jit(solution)/shard_map/suffix/pallas_call | solution.py:528
  105.5 12.1 %shard_map.119.refs_2_ = bf16[256,320]{1,0:T(8,128)(2,1)S(1)} custom-call(s32[1]{0:T(128)} %get-tuple-element.127.refs_1_.refs_0_, bf16[5,512,128]{2,1,0:T(8,128)(2,1)S(1)} %get-tuple-element.128.refs_2_.refs_1_, f32[5,512,128]{2,1,0:T(8,128)S(1)} %suffix.1.refs_2_, bf16[5,1024,128]{2,1,0:T(8,128)(2,1)S(1)} %copy-done.12), custom_call_target="tpu_custom_call" | custom-call | flops 671088640 | bytes 8000000 | tf_op jit(solution)/shard_map/pallas_call | solution.py:546
  117.6 2.6 %collective-permute-start.31 = (bf16[256,320]{1,0:T(8,128)(2,1)S(1)}, bf16[256,320]{1,0:T(8,128)(2,1)}, u32[]{:S(2)}, u32[]{:S(2)}) collective-permute-start(bf16[256,320]{1,0:T(8,128)(2,1)S(1)} %shard_map.119.refs_2_), channel_id=1, source_target_pairs={{0,2},{1,3},{2,0},{3,1},{4,6},{5,7},{6,4},{7,5},{8,10},{9,11},{10,... | collective-permute-start | bytes 491528 | tf_op jit(solution)/shard_map/ppermute | solution.py:399
  120.5 11.9 %shard_map.118.refs_2_ = bf16[256,320]{1,0:T(8,128)(2,1)S(1)} custom-call(s32[1]{0:T(128)} %get-tuple-element.127.refs_1_.refs_0_, bf16[5,512,128]{2,1,0:T(8,128)(2,1)S(1)} %get-tuple-element.128.refs_2_.refs_1_, f32[5,512,128]{2,1,0:T(8,128)S(1)} %suffix.1.refs_2_, bf16[5,1024,128]{2,1,0:T(8,128)(2,1)S(1)} %copy-done.12), custom_call_target="tpu_custom_call" | custom-call | flops 671088640 | bytes 8000000 | tf_op jit(solution)/shard_map/pallas_call | solution.py:546
  134.2 6.1 %collective-permute-done.25.refs_4_ = bf16[256,320]{1,0:T(8,128)(2,1)S(1)} collective-permute-done((bf16[256,320]{1,0:T(8,128)(2,1)S(1)}, bf16[256,320]{1,0:T(8,128)(2,1)S(1)}, u32[]{:S(2)}, u32[]{:S(2)}) %collective-permute-start.25) | collective-permute-done | bytes 163872 | tf_op jit(solution)/shard_map/ppermute | solution.py:399
  142.3 4.4 %shard_map.120.refs_12_ = bf16[320,512]{1,0:T(8,128)(2,1)} custom-call(s32[1]{0:T(128)S(6)} %copy.18.refs_0_, s32[1]{0:T(128)} %bitcast.refs_1_, bf16[256,320]{1,0:T(8,128)(2,1)S(1)} %shard_map.119.refs_2_, bf16[256,320]{1,0:T(8,128)(2,1)S(1)} %copy-done.3, bf16[256,320]{1,0:T(8,128)(2,1)} %collective-permute-done.31.refs_4_, ...), custom_call_target="tpu_custom_call" | custom-call | flops 838860800 | bytes 6000000 | tf_op jit(solution)/shard_map/pallas_call | solution.py:574
  146.7 4.4 %shard_map.121 = bf16[320,512]{1,0:T(8,128)(2,1)} custom-call(s32[1]{0:T(128)S(6)} %copy.18.refs_0_, s32[1]{0:T(128)} %bitcast.refs_1_, bf16[256,320]{1,0:T(8,128)(2,1)S(1)} %shard_map.118.refs_2_, bf16[256,320]{1,0:T(8,128)(2,1)} %collective-permute-done.24.refs_3_, ...), custom_call_target="tpu_custom_call", output_to_operand_aliasing={{}: (12, {})} | custom-call | flops 838860800 | bytes 6000000 | tf_op jit(solution)/shard_map/pallas_call | solution.py:574
  (77 shorter events, 14.9 us)
Async XLA Ops:
  2.3 9.0 %collective-permute-start.7 = (bf16[6,64,128]{2,1,0:T(8,128)(2,1)}, bf16[6,64,128]{2,1,0:T(8,128)(2,1)S(1)}, u32[]{:S(2)}, u32[]{:S(2)}) collective-permute-start(bf16[6,64,128]{2,1,0:T(8,128)(2,1)} %get-tuple-element.133.a_ref), channel_id=1, source_target_pairs={{128,0},{132,4},{136,8},{140,12},{144,16},{148,20},{152,24},{156,2... | collective-permute-start | bytes 294920 | tf_op jit(solution)/shard_map/ppermute | solution.py:34
  4.5 9.3 %collective-permute-start.8 = (bf16[6,64,128]{2,1,0:T(8,128)(2,1)}, bf16[6,64,128]{2,1,0:T(8,128)(2,1)S(1)}, u32[]{:S(2)}, u32[]{:S(2)}) collective-permute-start(bf16[6,64,128]{2,1,0:T(8,128)(2,1)} %get-tuple-element.133.a_ref), channel_id=1, source_target_pairs={{64,0},{68,4},{72,8},{76,12},{80,16},{84,20},{88,24},{92,28},{96,3... | collective-permute-start | bytes 294920 | tf_op jit(solution)/shard_map/ppermute | solution.py:34
  11.4 8.8 %collective-permute-start.9 = (bf16[6,64,128]{2,1,0:T(8,128)(2,1)}, bf16[6,64,128]{2,1,0:T(8,128)(2,1)S(1)}, u32[]{:S(2)}, u32[]{:S(2)}) collective-permute-start(bf16[6,64,128]{2,1,0:T(8,128)(2,1)} %get-tuple-element.133.a_ref), channel_id=1, source_target_pairs={{192,0},{196,4},{200,8},{204,12},{208,16},{212,20},{216,24},{220,2... | collective-permute-start | bytes 294920 | tf_op jit(solution)/shard_map/ppermute | solution.py:34
  21.1 36.0 %copy-start.13 = (bf16[4,6,32,128]{3,2,1,0:T(8,128)(2,1)}, bf16[4,6,32,128]{3,2,1,0:T(8,128)(2,1)S(1)}, u32[]{:S(2)}) copy-start(bf16[4,6,32,128]{3,2,1,0:T(8,128)(2,1)S(1)} %get-tuple-element.134.refs_2_) | copy-start | bytes 589828
  21.1 36.0 %copy-start.14 = (bf16[4,6,32,128]{3,2,1,0:T(8,128)(2,1)}, bf16[4,6,32,128]{3,2,1,0:T(8,128)(2,1)S(1)}, u32[]{:S(2)}) copy-start(bf16[4,6,32,128]{3,2,1,0:T(8,128)(2,1)S(1)} %get-tuple-element.136.refs_7_) | copy-start | bytes 589828
  21.1 8.8 %collective-permute-start.12 = (bf16[2,6,32,128]{3,2,1,0:T(8,128)(2,1)S(1)}, bf16[2,6,32,128]{3,2,1,0:T(8,128)(2,1)S(1)}, u32[]{:S(2)}, u32[]{:S(2)}) collective-permute-start(bf16[2,6,32,128]{3,2,1,0:T(8,128)(2,1)S(1)} %get-tuple-element.135), channel_id=1, source_target_pairs={{96,0},{100,4},{104,8},{108,12},{112,16},{116,20},{120,24},{124,28... | collective-permute-start | bytes 294920 | tf_op jit(solution)/shard_map/ppermute | solution.py:34
  22.3 8.0 %collective-permute-start.13 = (bf16[2,6,32,128]{3,2,1,0:T(8,128)(2,1)S(1)}, bf16[2,6,32,128]{3,2,1,0:T(8,128)(2,1)S(1)}, u32[]{:S(2)}, u32[]{:S(2)}) collective-permute-start(bf16[2,6,32,128]{3,2,1,0:T(8,128)(2,1)S(1)} %get-tuple-element.135), channel_id=1, source_target_pairs={{32,0},{36,4},{40,8},{44,12},{48,16},{52,20},{56,24},{60,28},{64,3... | collective-permute-start | bytes 294920 | tf_op jit(solution)/shard_map/ppermute | solution.py:34
  25.5 10.0 %collective-permute-start.14 = (bf16[4,6,32,128]{3,2,1,0:T(8,128)(2,1)S(1)}, bf16[4,6,32,128]{3,2,1,0:T(8,128)(2,1)S(1)}, u32[]{:S(2)}, u32[]{:S(2)}) collective-permute-start(bf16[4,6,32,128]{3,2,1,0:T(8,128)(2,1)S(1)} %get-tuple-element.136.refs_7_), channel_id=1, source_target_pairs={{4,0},{8,4},{12,8},{0,12},{20,16},{24,20},{28,24},{16,28},{36,32},... | collective-permute-start | bytes 589832 | tf_op jit(solution)/shard_map/ppermute | solution.py:34
  28.2 8.6 %collective-permute-start.15 = (bf16[4,6,32,128]{3,2,1,0:T(8,128)(2,1)S(1)}, bf16[4,6,32,128]{3,2,1,0:T(8,128)(2,1)S(1)}, u32[]{:S(2)}, u32[]{:S(2)}) collective-permute-start(bf16[4,6,32,128]{3,2,1,0:T(8,128)(2,1)S(1)} %get-tuple-element.136.refs_7_), channel_id=1, source_target_pairs={{12,0},{0,4},{4,8},{8,12},{28,16},{16,20},{20,24},{24,28},{44,32},... | collective-permute-start | bytes 589832 | tf_op jit(solution)/shard_map/ppermute | solution.py:34
  28.2 8.6 %collective-permute-start.16 = (bf16[4,6,32,128]{3,2,1,0:T(8,128)(2,1)S(1)}, bf16[4,6,32,128]{3,2,1,0:T(8,128)(2,1)S(1)}, u32[]{:S(2)}, u32[]{:S(2)}) collective-permute-start(bf16[4,6,32,128]{3,2,1,0:T(8,128)(2,1)S(1)} %get-tuple-element.136.refs_7_), channel_id=1, source_target_pairs={{8,0},{12,4},{0,8},{4,12},{24,16},{28,20},{16,24},{20,28},{40,32},... | collective-permute-start | bytes 589832 | tf_op jit(solution)/shard_map/ppermute | solution.py:34
  29.9 7.0 %collective-permute-start.10 = (bf16[4,6,32,128]{3,2,1,0:T(8,128)(2,1)S(1)}, bf16[4,6,32,128]{3,2,1,0:T(8,128)(2,1)S(1)}, u32[]{:S(2)}, u32[]{:S(2)}) collective-permute-start(bf16[4,6,32,128]{3,2,1,0:T(8,128)(2,1)S(1)} %get-tuple-element.134.refs_2_), channel_id=1, source_target_pairs={{16,0},{20,4},{24,8},{28,12},{32,16},{36,20},{40,24},{44,28},{48,3... | collective-permute-start | bytes 589832 | tf_op jit(solution)/shard_map/ppermute | solution.py:34
  30.3 26.8 %copy-start.20 = (bf16[2,6,32,128]{3,2,1,0:T(8,128)(2,1)}, bf16[2,6,32,128]{3,2,1,0:T(8,128)(2,1)S(1)}, u32[]{:S(2)}) copy-start(bf16[2,6,32,128]{3,2,1,0:T(8,128)(2,1)S(1)} %collective-permute-done.13.refs_6_) | copy-start | bytes 294916
  30.3 6.6 %collective-permute-start.11 = (bf16[4,6,32,128]{3,2,1,0:T(8,128)(2,1)S(1)}, bf16[4,6,32,128]{3,2,1,0:T(8,128)(2,1)S(1)}, u32[]{:S(2)}, u32[]{:S(2)}) collective-permute-start(bf16[4,6,32,128]{3,2,1,0:T(8,128)(2,1)S(1)} %get-tuple-element.134.refs_2_), channel_id=1, source_target_pairs={{112,0},{116,4},{120,8},{124,12},{0,16},{4,20},{8,24},{12,28},{16,... | collective-permute-start | bytes 589832 | tf_op jit(solution)/shard_map/ppermute | solution.py:34
  38.5 6.3 %collective-permute-start.22 = (bf16[4,5,32,128]{3,2,1,0:T(8,128)(2,1)S(1)}, bf16[4,5,32,128]{3,2,1,0:T(8,128)(2,1)S(1)}, u32[]{:S(2)}, u32[]{:S(2)}) collective-permute-start(bf16[4,5,32,128]{3,2,1,0:T(8,128)(2,1)S(1)} %get-tuple-element.144), channel_id=1, source_target_pairs={{32,0},{36,4},{40,8},{44,12},{48,16},{52,20},{56,24},{60,28},{64,3... | collective-permute-start | bytes 491528 | tf_op jit(solution)/shard_map/ppermute | solution.py:34
  40.8 8.1 %collective-permute-start.23 = (bf16[4,5,32,128]{3,2,1,0:T(8,128)(2,1)S(1)}, bf16[4,5,32,128]{3,2,1,0:T(8,128)(2,1)S(1)}, u32[]{:S(2)}, u32[]{:S(2)}) collective-permute-start(bf16[4,5,32,128]{3,2,1,0:T(8,128)(2,1)S(1)} %get-tuple-element.145), channel_id=1, source_target_pairs={{96,0},{100,4},{104,8},{108,12},{112,16},{116,20},{120,24},{124,28... | collective-permute-start | bytes 491528 | tf_op jit(solution)/shard_map/ppermute | solution.py:34
  40.9 8.7 %collective-permute-start.17 = (bf16[8,5,32,128]{3,2,1,0:T(8,128)(2,1)S(1)}, bf16[8,5,32,128]{3,2,1,0:T(8,128)(2,1)S(1)}, u32[]{:S(2)}, u32[]{:S(2)}) collective-permute-start(bf16[8,5,32,128]{3,2,1,0:T(8,128)(2,1)S(1)} %get-tuple-element.138), channel_id=1, source_target_pairs={{4,0},{8,4},{12,8},{0,12},{20,16},{24,20},{28,24},{16,28},{36,32},... | collective-permute-start | bytes 983048 | tf_op jit(solution)/shard_map/ppermute | solution.py:34
  42.1 11.4 %collective-permute-start.18 = (bf16[8,5,32,128]{3,2,1,0:T(8,128)(2,1)S(1)}, bf16[8,5,32,128]{3,2,1,0:T(8,128)(2,1)S(1)}, u32[]{:S(2)}, u32[]{:S(2)}) collective-permute-start(bf16[8,5,32,128]{3,2,1,0:T(8,128)(2,1)S(1)} %get-tuple-element.139), channel_id=1, source_target_pairs={{12,0},{0,4},{4,8},{8,12},{28,16},{16,20},{20,24},{24,28},{44,32},... | collective-permute-start | bytes 983048 | tf_op jit(solution)/shard_map/ppermute | solution.py:34
  42.4 11.1 %collective-permute-start.19 = (bf16[8,5,32,128]{3,2,1,0:T(8,128)(2,1)S(1)}, bf16[8,5,32,128]{3,2,1,0:T(8,128)(2,1)S(1)}, u32[]{:S(2)}, u32[]{:S(2)}) collective-permute-start(bf16[8,5,32,128]{3,2,1,0:T(8,128)(2,1)S(1)} %get-tuple-element.140), channel_id=1, source_target_pairs={{8,0},{12,4},{0,8},{4,12},{24,16},{28,20},{16,24},{20,28},{40,32},... | collective-permute-start | bytes 983048 | tf_op jit(solution)/shard_map/ppermute | solution.py:34
  44.7 8.7 %collective-permute-start.20 = (bf16[8,5,32,128]{3,2,1,0:T(8,128)(2,1)S(1)}, bf16[8,5,32,128]{3,2,1,0:T(8,128)(2,1)S(1)}, u32[]{:S(2)}, u32[]{:S(2)}) collective-permute-start(bf16[8,5,32,128]{3,2,1,0:T(8,128)(2,1)S(1)} %get-tuple-element.142), channel_id=1, source_target_pairs={{16,0},{20,4},{24,8},{28,12},{32,16},{36,20},{40,24},{44,28},{48,3... | collective-permute-start | bytes 983048 | tf_op jit(solution)/shard_map/ppermute | solution.py:34
  48.9 8.2 %collective-permute-start.21 = (bf16[8,5,32,128]{3,2,1,0:T(8,128)(2,1)S(1)}, bf16[8,5,32,128]{3,2,1,0:T(8,128)(2,1)S(1)}, u32[]{:S(2)}, u32[]{:S(2)}) collective-permute-start(bf16[8,5,32,128]{3,2,1,0:T(8,128)(2,1)S(1)} %get-tuple-element.143), channel_id=1, source_target_pairs={{112,0},{116,4},{120,8},{124,12},{0,16},{4,20},{8,24},{12,28},{16,... | collective-permute-start | bytes 983048 | tf_op jit(solution)/shard_map/ppermute | solution.py:34
  57.1 26.3 %copy-start = (bf16[1,512,1280]{2,1,0:T(8,128)(2,1)S(1)}, bf16[1,512,1280]{2,1,0:T(8,128)(2,1)}, u32[]{:S(2)}) copy-start(bf16[1,512,1280]{2,1,0:T(8,128)(2,1)} %param.14) | copy-start | bytes 3932164
  57.2 26.3 %copy-start.5 = (f32[5,64]{1,0:T(8,128)S(1)}, f32[5,64]{1,0:T(8,128)}, u32[]{:S(2)}) copy-start(f32[5,64]{1,0:T(8,128)} %refs_4_.1) | copy-start | bytes 3844
  60.7 14.2 %collective-permute-start.28 = (bf16[320,1280]{1,0:T(8,128)(2,1)S(1)}, bf16[320,1280]{1,0:T(8,128)(2,1)S(1)}, u32[]{:S(2)}, u32[]{:S(2)}) collective-permute-start(bf16[320,1280]{1,0:T(8,128)(2,1)S(1)} %copy-done.1), channel_id=1, source_target_pairs={{0,2},{1,3},{2,0},{3,1},{4,6},{5,7},{6,4},{7,5},{8,10},{9,11},{10,... | collective-permute-start | bytes 2457608 | tf_op jit(solution)/shard_map/ppermute | solution.py:399
  63.2 78.2 %collective-permute-start.27 = (bf16[320,1280]{1,0:T(8,128)(2,1)S(1)}, bf16[320,1280]{1,0:T(8,128)(2,1)}, u32[]{:S(2)}, u32[]{:S(2)}) collective-permute-start(bf16[320,1280]{1,0:T(8,128)(2,1)S(1)} %copy-done.1), channel_id=1, source_target_pairs={{0,1},{1,0},{2,3},{3,2},{4,5},{5,4},{6,7},{7,6},{8,9},{9,8},{10,11... | collective-permute-start | bytes 2457608 | tf_op jit(solution)/shard_map/ppermute | solution.py:399
  74.8 66.5 %collective-permute-start.29 = (bf16[320,1280]{1,0:T(8,128)(2,1)S(1)}, bf16[320,1280]{1,0:T(8,128)(2,1)}, u32[]{:S(2)}, u32[]{:S(2)}) collective-permute-start(bf16[320,1280]{1,0:T(8,128)(2,1)S(1)} %collective-permute-done.28.refs_8_), channel_id=1, source_target_pairs={{0,1},{1,0},{2,3},{3,2},{4,5},{5,4},{6,7},{7,6},{8,9},{9,8},{10,11... | collective-permute-start | bytes 2457608 | tf_op jit(solution)/shard_map/ppermute | solution.py:399
  117.6 23.7 %copy-start.21 = (f32[1280]{0:T(1024)S(1)}, f32[1280]{0:T(1024)}, u32[]{:S(2)}) copy-start(f32[1280]{0:T(1024)} %param.24) | copy-start | bytes 15364
  117.6 15.3 %collective-permute-start.31 = (bf16[256,320]{1,0:T(8,128)(2,1)S(1)}, bf16[256,320]{1,0:T(8,128)(2,1)}, u32[]{:S(2)}, u32[]{:S(2)}) collective-permute-start(bf16[256,320]{1,0:T(8,128)(2,1)S(1)} %shard_map.119.refs_2_), channel_id=1, source_target_pairs={{0,2},{1,3},{2,0},{3,1},{4,6},{5,7},{6,4},{7,5},{8,10},{9,11},{10,... | collective-permute-start | bytes 491528 | tf_op jit(solution)/shard_map/ppermute | solution.py:399
  120.2 13.2 %collective-permute-start.30 = (bf16[256,320]{1,0:T(8,128)(2,1)S(1)}, bf16[256,320]{1,0:T(8,128)(2,1)S(1)}, u32[]{:S(2)}, u32[]{:S(2)}) collective-permute-start(bf16[256,320]{1,0:T(8,128)(2,1)S(1)} %shard_map.119.refs_2_), channel_id=1, source_target_pairs={{0,1},{1,0},{2,3},{3,2},{4,5},{5,4},{6,7},{7,6},{8,9},{9,8},{10,11... | collective-permute-start | bytes 491528 | tf_op jit(solution)/shard_map/ppermute | solution.py:399
  132.4 7.8 %collective-permute-start.25 = (bf16[256,320]{1,0:T(8,128)(2,1)S(1)}, bf16[256,320]{1,0:T(8,128)(2,1)S(1)}, u32[]{:S(2)}, u32[]{:S(2)}) collective-permute-start(bf16[256,320]{1,0:T(8,128)(2,1)S(1)} %shard_map.118.refs_2_), channel_id=1, source_target_pairs={{0,2},{1,3},{2,0},{3,1},{4,6},{5,7},{6,4},{7,5},{8,10},{9,11},{10,... | collective-permute-start | bytes 491528 | tf_op jit(solution)/shard_map/ppermute | solution.py:399
  132.9 8.4 %collective-permute-start.32 = (bf16[256,320]{1,0:T(8,128)(2,1)}, bf16[256,320]{1,0:T(8,128)(2,1)}, u32[]{:S(2)}, u32[]{:S(2)}) collective-permute-start(bf16[256,320]{1,0:T(8,128)(2,1)} %collective-permute-done.31.refs_4_), channel_id=1, source_target_pairs={{0,1},{1,0},{2,3},{3,2},{4,5},{5,4},{6,7},{7,6},{8,9},{9,8},{10,11... | collective-permute-start | bytes 491528 | tf_op jit(solution)/shard_map/ppermute | solution.py:399
  134.1 12.6 %collective-permute-start.24 = (bf16[256,320]{1,0:T(8,128)(2,1)S(1)}, bf16[256,320]{1,0:T(8,128)(2,1)}, u32[]{:S(2)}, u32[]{:S(2)}) collective-permute-start(bf16[256,320]{1,0:T(8,128)(2,1)S(1)} %shard_map.118.refs_2_), channel_id=1, source_target_pairs={{0,1},{1,0},{2,3},{3,2},{4,5},{5,4},{6,7},{7,6},{8,9},{9,8},{10,11... | collective-permute-start | bytes 491528 | tf_op jit(solution)/shard_map/ppermute | solution.py:399
  140.2 6.5 %collective-permute-start.26 = (bf16[256,320]{1,0:T(8,128)(2,1)S(1)}, bf16[256,320]{1,0:T(8,128)(2,1)}, u32[]{:S(2)}, u32[]{:S(2)}) collective-permute-start(bf16[256,320]{1,0:T(8,128)(2,1)S(1)} %collective-permute-done.25.refs_4_), channel_id=1, source_target_pairs={{0,1},{1,0},{2,3},{3,2},{4,5},{5,4},{6,7},{7,6},{8,9},{9,8},{10,11... | collective-permute-start | bytes 491528 | tf_op jit(solution)/shard_map/ppermute | solution.py:399
  (16 other events, 130.9 us)
